TPU v7x, 32 devices: a whole 2x2x4 slice. The times are simulated.
32 devices in a mesh: pp: 4 (over y, x), cp: 4 (over z), tp: 2 (over core).
Axes of the slice: x: 2, y: 2, z: 4, core: 2. Of those that a mesh axis runs over, the one named last changes fastest.
Arguments:
- queries: bfloat16 [2048, 16384], P(('pp', 'cp'), 'tp'), may hold values from -12 to 12
- keys: bfloat16 [2048, 1024], P(('pp', 'cp'), 'tp'), may hold values from -12 to 12
- values: bfloat16 [2048, 1024], P(('pp', 'cp'), 'tp'), may hold values from -6 to 6
- pair_order: int32 [4, 4], replicated, may hold values from 0 to 3, each once within a row
- lengths: int32 [4, 2], replicated, may hold values from 128 to 256
- routes: int32 [4, 512, 1], P(None, 'cp'), may hold values from 0 to 7; in each aligned block of 128 rows (0 to 127, 128 to 255, ..., all dimensions but the last counted through in order) at most 32 rows name the same one
Outputs:
- rebalanced: bfloat16 [4096, 16384], P(('pp', 'cp', 'tp'))
Inputs may be any that keep to these rules, and one draw needn't show every extreme that they name: `routes`: at most 32 rows of one device's block name the same destination, and in some block one destination is named by exactly 32 rows.
All inputs are finite; a program needn't handle non-finite values.
Results may differ from a plain program's by a relative error of at most 0.003.
Values may be sent and summed in bfloat16 or wider, within the bound.
No kernel may reach another device: no remote copies, remote signals or barrier semaphores. Data moves between devices by JAX's collectives and lax.ppermute only.
A program may use at most 64 MiB of HBM per device.

v0:
```python
import jax
import jax.numpy as jnp
from jax import lax
from jax.sharding import PartitionSpec as P

HD = 128


masked_score = -1e30


def shifted(block, axis, distance):
    devices = range(lax.axis_size(axis))
    route = [((i - distance) % len(devices), i) for i in devices]
    return lax.ppermute(block, axis, route)


def pair_positions(pair_ids, block_len, cycle_size):
    offsets = jnp.arange(block_len, dtype=jnp.int32)
    first_half = pair_ids[:, None] * block_len + offsets[None, :]
    second_half = (2 * cycle_size - 1 - pair_ids)[:, None] * block_len + offsets[None, :]
    return jnp.concatenate([first_half, second_half], axis=1)


def dispatch_rows(attended, targets, dest_count, capacity):
    row_count = attended.shape[0]
    matches = targets[:, None] == jnp.arange(dest_count, dtype=jnp.int32)[None, :]
    row_ids = jnp.arange(row_count, dtype=jnp.int32)
    earlier = (row_ids[None, :] < row_ids[:, None]).astype(jnp.bfloat16)
    before = jnp.dot(earlier, matches.astype(jnp.bfloat16), preferred_element_type=jnp.float32)
    slot_index = jnp.sum(jnp.where(matches, before, 0.0), axis=1).astype(jnp.int32)
    slot_ids = jnp.arange(capacity, dtype=jnp.int32)
    picked_rows = jnp.logical_and(
        jnp.transpose(matches)[:, None, :], slot_index[None, None, :] == slot_ids[None, :, None]
    )
    selector = picked_rows.astype(jnp.bfloat16).reshape(dest_count * capacity, row_count)
    return jnp.dot(selector, attended, preferred_element_type=jnp.float32).astype(jnp.bfloat16)


def spread_rows(buffer, cycle_size, split_size, capacity, width):
    flat_buffer = buffer.reshape(cycle_size * split_size, capacity, width)
    moved = lax.all_to_all(flat_buffer, ("cp", "tp"), split_axis=0, concat_axis=0, tiled=True)
    moved = jnp.transpose(moved.reshape(cycle_size, split_size, capacity, width), (0, 2, 1, 3))
    return moved.reshape(cycle_size * capacity, split_size * width)


def arrange_rows(attended, routes, source, cycle_size, split_size):
    row_count, width = attended.shape
    dest_count = cycle_size * split_size
    capacity = 2 * row_count // dest_count
    targets = lax.dynamic_index_in_dim(routes, source, 0, keepdims=False)[:, 0]
    buffer = dispatch_rows(attended, targets, dest_count, capacity)
    buffer = buffer.reshape(cycle_size, split_size, capacity, width)
    return spread_rows(buffer, cycle_size, split_size, capacity, width)


def body(queries, keys, values, pair_order, lengths, routes):
    cycle_size = lax.axis_size("cp")
    split_size = lax.axis_size("tp")
    section = lax.axis_index("pp")
    place = lax.axis_index("cp")
    row_count = queries.shape[0]
    block_len = row_count // 4
    width = queries.shape[1]
    group_count = keys.shape[1] // HD
    group_size = width // keys.shape[1]
    score_scale = HD ** (-0.5)
    order_row = lax.dynamic_index_in_dim(pair_order, section, 0, keepdims=False)
    own_pair = lax.dynamic_index_in_dim(order_row, place, 0, keepdims=True)
    query_pos = pair_positions(own_pair, block_len, cycle_size).reshape(2 * block_len)
    limits = lax.dynamic_index_in_dim(lengths, section, 0, keepdims=False)
    query_rows = queries.reshape(2, 2 * block_len, group_count, group_size, HD)
    stat_shape = (2, 2 * block_len, group_count, group_size)
    start_state = (
        jnp.full(stat_shape, masked_score, jnp.float32),
        jnp.zeros(stat_shape, jnp.float32),
        jnp.zeros(stat_shape + (HD,), jnp.float32),
    )
    state = start_state
    key_piece = lax.all_gather(keys, "cp", axis=0, tiled=True)
    value_piece = lax.all_gather(values, "cp", axis=0, tiled=True)
    shard_count = key_piece.shape[0] // row_count
    first_shard = jnp.int32(0) // row_count
    for base in range(0, shard_count, 4):
        block = min(4, shard_count - base)
        key_block = key_piece[base * row_count : (base + block) * row_count].reshape(
            block, 2, 2 * block_len, group_count, HD
        )
        value_block = value_piece[base * row_count : (base + block) * row_count].reshape(
            block, 2, 2 * block_len, group_count, HD
        )
        shard_ids = first_shard + base + jnp.arange(block, dtype=jnp.int32)
        key_pos = pair_positions(order_row[shard_ids], block_len, cycle_size).reshape(
            block * 2 * block_len
        )
        allowed = jnp.logical_and(
            key_pos[None, None, :] <= query_pos[None, :, None],
            key_pos[None, None, :] < limits[:, None, None],
        )
        allowed = allowed[:, :, None, None, :]
        scores = jnp.einsum(
            "sqgrd,nskgd->sqgrnk", query_rows, key_block, preferred_element_type=jnp.float32
        )
        scores = scores.reshape(stat_shape + (block * 2 * block_len,)) * score_scale
        running_max, running_total, running_sum = state
        block_max = jnp.max(jnp.where(allowed, scores, masked_score), axis=4)
        new_max = jnp.maximum(running_max, block_max)
        weights = jnp.where(allowed, jnp.exp(scores - new_max[..., None]), 0.0)
        carry_factor = jnp.exp(running_max - new_max)
        running_total = running_total * carry_factor + jnp.sum(weights, axis=4)
        shaped = weights.astype(jnp.bfloat16).reshape(stat_shape + (block, 2 * block_len))
        running_sum = running_sum * carry_factor[..., None] + jnp.einsum(
            "sqgrnk,nskgd->sqgrd", shaped, value_block, preferred_element_type=jnp.float32
        )
        state = (new_max, running_total, running_sum)
    attended = (state[2] / state[1][..., None]).astype(jnp.bfloat16).reshape(row_count, width)
    arranged = arrange_rows(attended, routes, section, cycle_size, split_size)
    return shifted(arranged, "pp", 1)


def solution(mesh):
    placed = (
        P(("pp", "cp"), "tp"),
        P(("pp", "cp"), "tp"),
        P(("pp", "cp"), "tp"),
        P(),
        P(),
        P(None, "cp", None),
    )
    return jax.shard_map(
        body, mesh=mesh, in_specs=placed, out_specs=P(("pp", "cp", "tp"), None), check_vma=False
    )
```

profile of v0, /device:TPU:0, one launch (start us, length us, event | category | flops | bytes accessed | tf_op | source)
XLA Modules:
  0.0 287.3 jit_solution(959507155664328261)
XLA Ops:
  0.0 0.7 copy-done
  0.7 0.1 fusion.9
  0.9 0.7 fusion.14
  1.6 1.3 dynamic_slice.18
  4.1 0.6 gather_fusion
  4.8 0.9 dynamic-slice_reduce_fusion
  6.1 2.2 copy.30
  8.3 17.4 %all_gather.6 = bf16[512,512]{1,0:T(8,128)(2,1)S(1)} all-gather(bf16[128,512]{1,0:T(8,128)(2,1)S(1)} %copy-done.2), channel_id=1, replica_groups=mesh['pp'=4,'cp'=4,'tp'=2] {'cp'}, dimensions={0}, use_global_device_ids=true | all-gather | bytes 655360 | tf_op jit(solution)/shard_map/all_gather | solution.py:80
  25.8 0.1 broadcast_and_fusion
  25.9 5.5 %fusion = (f32[2,64,4,16]{1,3,2,0:T(8,128)S(1)}, f32[2,4,4,64,64,16]{4,3,5,2,1,0:T(8,128)S(1)}) fusion(pred[2,64,4,64]{1,3,2,0:T(8,128)(4,1)S(1)} %broadcast_and_fusion, bf16[2,64,4,16,128,1]{4,3,2,1,0,5:T(8,128)(2,1)S(1)} %bitcast.52, bf16[4,2,64,4,128,1]{4,3,2,1,0,5:T(4,128)(2,1)S(1)} %bitcast.54), kind=kOutput, calls=%fused_computation.3 | convolution fusion | flops 543154176 | bytes 11075584 | tf_op jit(solution)/shard_map/sqgrd,nskgd->sqgrnk/dot_general | solution.py:101
  31.4 6.2 %fusion.3 = (f32[2,64,4,16]{1,3,2,0:T(8,128)S(1)}, bf16[2,64,4,16,4,64]{1,5,3,4,2,0:T(8,128)(2,1)}) fusion(f32[2,4,4,64,64,16]{4,3,5,2,1,0:T(8,128)S(1)} %get-tuple-element.12, f32[2,64,4,16]{1,3,2,0:T(8,128)S(1)} %broadcast_maximum_fusion, pred[2,64,4,64]{1,3,2,0:T(8,128)(4,1)S(1)} %broadcast_and_fusion), kind=kLoop, calls=%fused_computation.6 | loop fusion | flops 10477568 | bytes 12681216 | tf_op jit(solution)/shard_map/reduce_sum | solution.py:110
  37.8 0.1 copy.17
  38.0 17.2 %copy.15 = bf16[2,64,4,16,4,64]{5,3,4,1,2,0:T(8,128)(2,1)} copy(bf16[2,64,4,16,4,64]{1,5,3,4,2,0:T(8,128)(2,1)} %get-tuple-element.6) | data formatting | bytes 8388608 | tf_op jit(solution)/shard_map/convert_element_type | solution.py:111
  55.2 16.2 %all_gather.7 = bf16[512,512]{1,0:T(8,128)(2,1)S(1)} all-gather(bf16[128,512]{1,0:T(8,128)(2,1)S(1)} %copy-done.3), channel_id=1, replica_groups=mesh['pp'=4,'cp'=4,'tp'=2] {'cp'}, dimensions={0}, use_global_device_ids=true | all-gather | bytes 655360 | tf_op jit(solution)/shard_map/all_gather | solution.py:81
  71.6 5.7 %fusion.6 = bf16[2,64,4,16,128]{4,3,1,2,0:T(8,128)(2,1)S(1)} fusion(bf16[2,64,4,16,4,64]{5,3,4,1,2,0:T(8,128)(2,1)} %copy.15, f32[2,64,4,16]{3,1,2,0:T(8,128)S(1)} %copy.17, f32[2,64,4,16]{3,1,2,0:T(8,128)S(1)} %copy.14, bf16[4,2,64,4,128,1]{4,3,2,1,0,5:T(4,128)(2,1)S(1)} %bitcast.56), kind=kOutput, calls=%fused_computation.11 | convolution fusion | flops 540016640 | bytes 6881280 | tf_op jit(solution)/shard_map/sqgrnk,nskgd->sqgrd/dot_general | solution.py:112
  77.3 1.9 copy.18
  79.2 2.8 reshape.237
  82.1 1.2 convolution_convert_fusion
  83.3 97.9 %all_to_all.5 = bf16[8,32,8192]{2,1,0:T(8,128)(2,1)S(1)} all-to-all(bf16[8,32,8192]{2,1,0:T(8,128)(2,1)S(1)} %bitcast.49), channel_id=1, replica_groups=mesh['pp'=4,'cp'=4,'tp'=2] {'cp','tp'}, dimensions={0} | all-to-all | bytes 8388608 | tf_op jit(solution)/shard_map/all_to_all | solution.py:42
  181.2 6.4 %copy.19 = bf16[4,2,32,8192]{3,1,2,0:T(2,128)(2,1)} copy(bf16[4,2,32,8192]{3,2,1,0:T(8,128)(2,1)S(1)} %bitcast.50) | data formatting | bytes 8388608 | tf_op jit(solution)/shard_map/reshape | solution.py:43
  187.6 4.8 %copy.31 = bf16[16,8,2,8192]{3,1,2,0:T(8,128)(2,1)S(1)} copy(bf16[16,8,2,8192]{3,2,1,0:T(2,128)(2,1)} %bitcast.51) | data formatting | bytes 8388608
  192.4 1.6 collective-permute-start
  194.0 91.3 %collective-permute-done = bf16[128,16384]{1,0:T(8,128)(2,1)S(1)} collective-permute-done((bf16[128,16384]{1,0:T(8,128)(2,1)S(1)}, bf16[128,16384]{1,0:T(8,128)(2,1)S(1)}, u32[]{:S(2)}, u32[]{:S(2)}) %collective-permute-start) | collective-permute-done | bytes 4194336 | tf_op jit(solution)/shard_map/ppermute | solution.py:15
  285.3 2.0 copy.45
  (26 shorter events, 0.9 us)
Async XLA Ops:
  0.0 0.7 copy-start
  0.0 8.3 %copy-start.2 = (bf16[128,512]{1,0:T(8,128)(2,1)S(1)}, bf16[128,512]{1,0:T(8,128)(2,1)}, u32[]{:S(2)}) copy-start(bf16[128,512]{1,0:T(8,128)(2,1)} %param.7) | copy-start | bytes 393220
  38.0 17.2 %copy-start.3 = (bf16[128,512]{1,0:T(8,128)(2,1)S(1)}, bf16[128,512]{1,0:T(8,128)(2,1)}, u32[]{:S(2)}) copy-start(bf16[128,512]{1,0:T(8,128)(2,1)} %param.8) | copy-start | bytes 393220
  192.4 94.9 %copy-start.1 = (s32[4,128,1]{1,2,0:T(1,128)S(1)}, s32[4,128,1]{1,2,0:T(1,128)}, u32[]{:S(2)}) copy-start(s32[4,128,1]{1,2,0:T(1,128)} %param.11) | copy-start | bytes 6148
  192.4 92.9 %collective-permute-start = (bf16[128,16384]{1,0:T(8,128)(2,1)S(1)}, bf16[128,16384]{1,0:T(8,128)(2,1)S(1)}, u32[]{:S(2)}, u32[]{:S(2)}) collective-permute-start(bf16[128,16384]{1,0:T(8,128)(2,1)S(1)} %bitcast.53), channel_id=1, source_target_pairs={{24,0},{0,8},{8,16},{16,24},{25,1},{1,9},{9,17},{17,25},{26,2},{2,... | collective-permute-start | bytes 12582920 | tf_op jit(solution)/shard_map/ppermute | solution.py:15
where the time goes:
time: 288 us; the launch traced here: 287 us
  blocking collectives  131 us (45%)
  waiting for transfers between devices  91.3 us (32%)
  local copies, waits for them, and re-layouts  42 us (15%)
  matrix products  12.6 us (4%)
  other arithmetic  6.85 us (2%)
    all_to_all x1, blocking collectives, spread_rows(): lax.all_to_all(flat_buffer, ('cp', 'tp'), split_axis=0, concat_axis=0, ti...  97.9 us
    ppermute x1, waiting for transfers between devices, shifted(): return lax.ppermute(block, axis, route)  91.3 us
    all_gather x1, blocking collectives, body(): key_piece = lax.all_gather(keys, 'cp', axis=0, tiled=True)  17.4 us
    convert_element_type x1, local copies, waits for them, and re-layouts, body(): weights.astype(jnp.bfloat16).reshape(stat_shape + (block, 2 * block_len))  17.2 us
    all_gather x1, blocking collectives, body(): value_piece = lax.all_gather(values, 'cp', axis=0, tiled=True)  16.2 us
    unnamed x11, local copies, waits for them, and re-layouts  9.69 us
    reshape x1, local copies, waits for them, and re-layouts, spread_rows(): moved.reshape(cycle_size, split_size, capacity, width)  6.38 us
    reduce_sum x1, other arithmetic, body(): running_total = running_total * carry_factor + jnp.sum(weights, axis=4)  6.22 us
  transfers between devices with their start and end apart: 1, of which 1 were waited for; matrix products, arithmetic and copies ran while one was open for 0% of the time, Pallas kernels for 0%

commit v1 on v0

--- a/solution.py
+++ b/solution.py
@@ -1,6 +1,8 @@
 import jax
 import jax.numpy as jnp
 from jax import lax
+from jax.experimental import pallas as pl
+from jax.experimental.pallas import tpu as pltpu
 from jax.sharding import PartitionSpec as P
 
 HD = 128
@@ -54,7 +56,7 @@
     return spread_rows(buffer, cycle_size, split_size, capacity, width)
 
 
-def body(queries, keys, values, pair_order, lengths, routes):
+def general_body(queries, keys, values, pair_order, lengths, routes):
     cycle_size = lax.axis_size("cp")
     split_size = lax.axis_size("tp")
     section = lax.axis_index("pp")
@@ -118,6 +120,297 @@
     return shifted(arranged, "pp", 1)
 
 
+def to_partner(block, mask):
+    size = lax.axis_size("cp")
+    return lax.ppermute(block, "cp", [(i, i ^ mask) for i in range(size)])
+
+
+def to_next_section(block, mask):
+    sections, size = lax.axis_size("pp"), lax.axis_size("cp")
+    route = [
+        (p * size + i, ((p + 1) % sections) * size + (i ^ mask))
+        for p in range(sections)
+        for i in range(size)
+    ]
+    return lax.ppermute(block, ("pp", "cp"), route)
+
+
+def row_to_column(row):
+    count = row.shape[1]
+    down = lax.broadcasted_iota(jnp.int32, (count, count), 0)
+    across = lax.broadcasted_iota(jnp.int32, (count, count), 1)
+    return jnp.sum(jnp.where(down == across, row, 0), axis=1, keepdims=True)
+
+
+def rank_in_row(row):
+    count = row.shape[1]
+    down = lax.broadcasted_iota(jnp.int32, (count, count), 0)
+    across = lax.broadcasted_iota(jnp.int32, (count, count), 1)
+    hits = jnp.logical_and(row_to_column(row) == row, down < across)
+    return jnp.sum(hits.astype(jnp.int32), axis=0, keepdims=True)
+
+
+def one_hot(rank, match, height):
+    ids = lax.broadcasted_iota(jnp.int32, (height, rank.shape[1]), 0)
+    return jnp.logical_and(ids == rank, match).astype(jnp.float32).astype(jnp.bfloat16)
+
+
+def make_ready(keys, values, route_rows, where, *, cycle_size, split_size, packed_rows):
+    row_count, width = keys.shape
+    sections = route_rows.shape[0]
+    head_rows = row_count + 16
+
+    def kernel(where_ref, k_ref, v_ref, r_ref, first_ref, rest_ref, pack_ref):
+        section, place = where_ref[0], where_ref[1]
+        first_ref[0:row_count, 0:HD] = k_ref[:, 0:HD]
+        first_ref[0:row_count, HD : 2 * HD] = v_ref[:, 0:HD]
+        spare = jnp.zeros((16 - sections, row_count), jnp.float32)
+        sent = jnp.concatenate([r_ref[...].astype(jnp.float32), spare], axis=0).astype(jnp.bfloat16)
+        first_ref[row_count:head_rows, 0:HD] = sent
+        first_ref[row_count:head_rows, HD : 2 * HD] = jnp.zeros((16, HD), jnp.bfloat16)
+        rest_ref[:, 0 : width - HD] = k_ref[:, HD:width]
+        rest_ref[:, width - HD :] = v_ref[:, HD:width]
+        chips = r_ref[pl.ds(section, 1), :] // split_size
+        rank = rank_in_row(chips)
+        for mask in range(cycle_size):
+            pack_ref[mask] = one_hot(rank, chips == (place ^ mask), packed_rows)
+
+    return pl.pallas_call(
+        kernel,
+        out_shape=(
+            jax.ShapeDtypeStruct((head_rows, 2 * HD), jnp.bfloat16),
+            jax.ShapeDtypeStruct((row_count, 2 * (width - HD)), jnp.bfloat16),
+            jax.ShapeDtypeStruct((cycle_size, packed_rows, row_count), jnp.bfloat16),
+        ),
+        in_specs=[pl.BlockSpec(memory_space=pltpu.SMEM)] + [pl.BlockSpec(memory_space=pltpu.VMEM)] * 3,
+        name="make_ready",
+    )(where, keys, values, route_rows)
+
+
+def make_unpack(route_rows, heads, where, *, cycle_size, split_size, packed_rows, capacity):
+    sections, row_count = route_rows.shape
+
+    def kernel(where_ref, r_ref, *refs):
+        head_refs, (own_ref, twin_ref) = refs[: cycle_size - 1], refs[cycle_size - 1 :]
+        place, core = where_ref[1], where_ref[2]
+        source = (where_ref[0] + sections - 1) % sections
+        for mask in range(cycle_size):
+            if mask == 0:
+                targets = r_ref[pl.ds(source, 1), :]
+            else:
+                block = head_refs[mask - 1][...].astype(jnp.float32)
+                ids = lax.broadcasted_iota(jnp.int32, block.shape, 0)
+                targets = jnp.sum(jnp.where(ids == source, block, 0.0), axis=0, keepdims=True)
+                targets = targets.astype(jnp.int32)
+            chips = targets // split_size
+            packed = one_hot(rank_in_row(chips), chips == place, packed_rows)
+            slots = rank_in_row(targets)
+            for ref, which in ((own_ref, core), (twin_ref, 1 - core)):
+                slotted = one_hot(slots, targets == place * split_size + which, capacity)
+                ref[mask] = lax.dot_general(
+                    slotted, packed, (((1,), (1,)), ((), ())), preferred_element_type=jnp.float32
+                ).astype(jnp.bfloat16)
+
+    shape = jax.ShapeDtypeStruct((cycle_size, capacity, packed_rows), jnp.bfloat16)
+    return pl.pallas_call(
+        kernel,
+        grid=(1,),
+        out_shape=(shape, shape),
+        in_specs=[
+            pl.BlockSpec(memory_space=pltpu.SMEM),
+            pl.BlockSpec(memory_space=pltpu.VMEM),
+        ]
+        + [pl.BlockSpec((16, HD), lambda i: (row_count // 16, 0))] * (cycle_size - 1),
+        name="make_unpack",
+    )(where, route_rows, *heads)
+
+
+def attend(queries, pieces, pack, pair_order, lengths, where, group, *, cycle_size, group_size):
+    row_count = queries.shape[0]
+    half = row_count // 2
+    block_len = half // 2
+    packed_rows = pack.shape[1]
+    step_heads = min(4, group_size)
+    steps = group_size // step_heads
+    tile = step_heads * HD
+    scale = HD ** (-0.5)
+
+    def kernel(where_ref, order_ref, len_ref, q_ref, *refs):
+        kv_refs, pack_ref, out_refs = refs[: 2 * cycle_size], refs[2 * cycle_size], refs[2 * cycle_size + 1 :]
+        section, place = where_ref[0], where_ref[1]
+        own = order_ref[section, place]
+        row = lax.broadcasted_iota(jnp.int32, (half, cycle_size * half), 0)
+        query_pos = jnp.where(row < block_len, own, 2 * cycle_size - 2 - own) * block_len + row
+        lane = lax.broadcasted_iota(jnp.int32, (half, half), 1)
+        key_pos = []
+        for mask in range(cycle_size):
+            pair = order_ref[section, place ^ mask]
+            key_pos.append(jnp.where(lane < block_len, pair, 2 * cycle_size - 2 - pair) * block_len + lane)
+        key_pos = jnp.concatenate(key_pos, axis=1)
+        causal = key_pos <= query_pos
+        parts = []
+        for seq in range(2):
+            rows = slice(seq * half, (seq + 1) * half)
+            allowed = jnp.logical_and(causal, key_pos < len_ref[section, seq])
+            offset = jnp.where(allowed, 0.0, masked_score)
+            offset = jnp.concatenate([offset] * step_heads, axis=0)
+            k = jnp.concatenate([kv_refs[2 * m][rows, :] for m in range(cycle_size)], axis=0)
+            v = jnp.concatenate([kv_refs[2 * m + 1][rows, :] for m in range(cycle_size)], axis=0)
+            q = jnp.concatenate([q_ref[rows, h * HD : (h + 1) * HD] for h in range(step_heads)], axis=0)
+            scores = lax.dot_general(q, k, (((1,), (1,)), ((), ())), preferred_element_type=jnp.float32)
+            scores = jnp.where(offset == 0.0, scores * scale, masked_score)
+            weights = jnp.exp(scores - jnp.max(scores, axis=1, keepdims=True))
+            total = jnp.sum(weights, axis=1, keepdims=True)
+            summed = jnp.dot(weights.astype(jnp.bfloat16), v, preferred_element_type=jnp.float32)
+            done = (summed / total).astype(jnp.bfloat16)
+            parts.append(
+                jnp.concatenate([done[h * half : (h + 1) * half] for h in range(step_heads)], axis=1)
+            )
+        attended = jnp.concatenate(parts, axis=0)
+        for mask in range(cycle_size):
+            out_refs[mask][...] = jnp.dot(
+                pack_ref[mask], attended, preferred_element_type=jnp.float32
+            ).astype(jnp.bfloat16)
+
+    kv_specs, kv_args = [], []
+    for key_array, key_col, value_array, value_col in pieces:
+        kv_specs.append(pl.BlockSpec((row_count, HD), lambda i, *_, col=key_col: (0, col)))
+        kv_specs.append(pl.BlockSpec((row_count, HD), lambda i, *_, col=value_col: (0, col)))
+        kv_args += [key_array, value_array]
+    return pl.pallas_call(
+        kernel,
+        grid_spec=pltpu.PrefetchScalarGridSpec(
+            num_scalar_prefetch=3,
+            grid=(steps,),
+            in_specs=[pl.BlockSpec((row_count, tile), lambda i, *_: (0, group * steps + i))]
+            + kv_specs
+            + [pl.BlockSpec(pack.shape, lambda i, *_: (0, 0, 0))],
+            out_specs=[pl.BlockSpec((packed_rows, tile), lambda i, *_: (0, i))] * cycle_size,
+        ),
+        out_shape=[jax.ShapeDtypeStruct((packed_rows, steps * tile), jnp.bfloat16)] * cycle_size,
+        name="attend",
+    )(where, pair_order, lengths, queries, *kv_args, pack)
+
+
+def unpack_rows(received, own_slots, twin_slots, where, out, group, *, group_count, split_size):
+    cycle_size, capacity, packed_rows = own_slots.shape
+    width = received[0].shape[1]
+    tile = min(512, width)
+    steps = width // tile
+    rows = cycle_size * capacity
+    full = split_size * group_count * width
+
+    def kernel(where_ref, *refs):
+        in_refs, own_ref, twin_ref = refs[:cycle_size], refs[cycle_size], refs[cycle_size + 1]
+        out_ref, send_ref = refs[-2:]
+        place = where_ref[1]
+        for mask in range(cycle_size):
+            block = in_refs[mask][...]
+            at = pl.ds(pl.multiple_of((place ^ mask) * capacity, capacity), capacity)
+            out_ref[at, :] = jnp.dot(own_ref[mask], block, preferred_element_type=jnp.float32).astype(jnp.bfloat16)
+            send_ref[at, :] = jnp.dot(twin_ref[mask], block, preferred_element_type=jnp.float32).astype(jnp.bfloat16)
+
+    slots_spec = pl.BlockSpec(own_slots.shape, lambda i, *_: (0, 0, 0))
+    in_specs = [pl.BlockSpec((packed_rows, tile), lambda i, *_: (0, i))] * cycle_size + [slots_spec] * 2
+    args = list(received) + [own_slots, twin_slots]
+    aliases = {}
+    if out is not None:
+        in_specs.append(pl.BlockSpec(memory_space=pl.ANY))
+        aliases = {len(args) + 1: 0}
+        args.append(out)
+    return pl.pallas_call(
+        kernel,
+        grid_spec=pltpu.PrefetchScalarGridSpec(
+            num_scalar_prefetch=1,
+            grid=(steps,),
+            in_specs=in_specs,
+            out_specs=[
+                pl.BlockSpec((rows, tile), lambda i, w: (0, (w[2] * group_count + group) * steps + i)),
+                pl.BlockSpec((rows, tile), lambda i, w: (0, i)),
+            ],
+        ),
+        out_shape=[
+            jax.ShapeDtypeStruct((rows, full), jnp.bfloat16),
+            jax.ShapeDtypeStruct((rows, width), jnp.bfloat16),
+        ],
+        input_output_aliases=aliases,
+        name="unpack_rows",
+    )(where, *args)
+
+
+def place_twin(block, out, where, group, *, group_count):
+    rows, width = block.shape
+    tile = min(512, width)
+    steps = width // tile
+
+    def kernel(where_ref, in_ref, old_ref, out_ref):
+        out_ref[...] = in_ref[...]
+
+    return pl.pallas_call(
+        kernel,
+        grid_spec=pltpu.PrefetchScalarGridSpec(
+            num_scalar_prefetch=1,
+            grid=(steps,),
+            in_specs=[pl.BlockSpec((rows, tile), lambda i, w: (0, i)), pl.BlockSpec(memory_space=pl.ANY)],
+            out_specs=pl.BlockSpec((rows, tile), lambda i, w: (0, ((1 - w[2]) * group_count + group) * steps + i)),
+        ),
+        out_shape=jax.ShapeDtypeStruct(out.shape, out.dtype),
+        input_output_aliases={2: 0},
+        name="place_twin",
+    )(where, block, out)
+
+
+def body(queries, keys, values, pair_order, lengths, routes):
+    cycle_size = lax.axis_size("cp")
+    split_size = lax.axis_size("tp")
+    row_count, width = queries.shape
+    group_count = keys.shape[1] // HD
+    group_size = width // keys.shape[1]
+    dest_count = cycle_size * split_size
+    capacity = 2 * row_count // dest_count
+    packed_rows = min(row_count, split_size * capacity)
+    masks = [2, 3, 1, 0]
+    where = jnp.stack([lax.axis_index("pp"), lax.axis_index("cp"), lax.axis_index("tp")]).astype(jnp.int32)
+    route_rows = routes[:, :, 0]
+    head, rest, pack = make_ready(
+        keys, values, route_rows, where, cycle_size=cycle_size, split_size=split_size, packed_rows=packed_rows
+    )
+    heads = {mask: to_partner(head, mask) for mask in masks if mask}
+    rests = {mask: to_partner(rest, mask) for mask in masks if mask}
+    own_slots, twin_slots = make_unpack(
+        route_rows,
+        [heads[mask] for mask in range(1, cycle_size)],
+        where,
+        cycle_size=cycle_size,
+        split_size=split_size,
+        packed_rows=packed_rows,
+        capacity=capacity,
+    )
+    arrived = []
+    for group in range(group_count):
+        pieces = [(keys, group, values, group)]
+        for mask in range(1, cycle_size):
+            if group == 0:
+                pieces.append((heads[mask], 0, heads[mask], 1))
+            else:
+                pieces.append((rests[mask], group - 1, rests[mask], group_count + group - 2))
+        packed = attend(
+            queries, pieces, pack, pair_order, lengths, where, group, cycle_size=cycle_size, group_size=group_size
+        )
+        sent = {mask: to_next_section(packed[mask], mask) for mask in masks}
+        arrived.append([sent[mask] for mask in range(cycle_size)])
+    out = None
+    twins = []
+    for group in range(group_count):
+        out, send = unpack_rows(
+            arrived[group], own_slots, twin_slots, where, out, group, group_count=group_count, split_size=split_size
+        )
+        twins.append(lax.ppermute(send, "tp", [(0, 1), (1, 0)]))
+    for group in range(group_count):
+        out = place_twin(twins[group], out, where, group, group_count=group_count)
+    return out
+
+
 def solution(mesh):
     placed = (
         P(("pp", "cp"), "tp"),
@@ -127,6 +420,11 @@
         P(),
         P(None, "cp", None),
     )
+    small = mesh.shape["cp"] == 4 and mesh.shape["tp"] == 2
     return jax.shard_map(
-        body, mesh=mesh, in_specs=placed, out_specs=P(("pp", "cp", "tp"), None), check_vma=False
-    )
+        body if small else general_body,
+        mesh=mesh,
+        in_specs=placed,
+        out_specs=P(("pp", "cp", "tp"), None),
+        check_vma=False,
+    )

time: 288 us -> 165 us (0.57)
  the two profiles are of different devices: /device:TPU:0 before, /device:TPU:3 now
where the time goes in v1:
time: 165 us; the launch traced here: 164 us
  starting transfers between devices  87.3 us (53%)
  Pallas kernels  61.3 us (37%)
  local copies, waits for them, and re-layouts  8.12 us (5%)
  waiting for transfers between devices  6.3 us (4%)
    ppermute x16, starting transfers between devices, to_next_section(): return lax.ppermute(block, ('pp', 'cp'), route)  57.2 us
    pallas_call x4, Pallas kernels, attend(): pl.pallas_call(kernel, grid_spec=pltpu.PrefetchScalarGridSpec(num_scalar_...  24.6 us
    ppermute x4, starting transfers between devices, body(): twins.append(lax.ppermute(send, 'tp', [(0, 1), (1, 0)]))  22.8 us
    pallas_call x4, Pallas kernels, unpack_rows(): pl.pallas_call(kernel, grid_spec=pltpu.PrefetchScalarGridSpec(num_scalar_...  17.7 us
    pallas_call x4, Pallas kernels, place_twin(): pl.pallas_call(kernel, grid_spec=pltpu.PrefetchScalarGridSpec(num_scalar_...  15.3 us
    unnamed x53, local copies, waits for them, and re-layouts  8.12 us
    ppermute x6, starting transfers between devices, to_partner(): return lax.ppermute(block, 'cp', [(i, i ^ mask) for i in range(size)])  7.24 us
    ppermute x6, waiting for transfers between devices, to_partner(): return lax.ppermute(block, 'cp', [(i, i ^ mask) for i in range(size)])  6.25 us
  transfers between devices with their start and end apart: 26, of which 3 were waited for; matrix products, arithmetic and copies ran while one was open for 1% of the time, Pallas kernels for 30%

profile of v1, /device:TPU:3, one launch (start us, length us, event | category | flops | bytes accessed | tf_op | source)
XLA Modules:
  0.0 163.7 jit_solution(15849391007321627298)
XLA Ops:
  8.5 2.6 %collective-permute-done.9.refs_2_.refs_6_.refs_7_ = bf16[144,256]{1,0:T(8,128)(2,1)S(1)} collective-permute-done((bf16[144,256]{1,0:T(8,128)(2,1)}, bf16[144,256]{1,0:T(8,128)(2,1)S(1)}, u32[]{:S(2)}, u32[]{:S(2)}) %collective-permute-start.9) | collective-permute-done | bytes 73760 | tf_op jit(solution)/shard_map/ppermute | solution.py:125
  11.8 6.1 %attend.7 = (bf16[64,2048]{1,0:T(8,128)(2,1)}, bf16[64,2048]{1,0:T(8,128)(2,1)}, bf16[64,2048]{1,0:T(8,128)(2,1)}, bf16[64,2048]{1,0:T(8,128)(2,1)}) custom-call(s32[3]{0:T(128)} %pad_add_fusion.where_ref, s32[4,4]{1,0:T(4,128)} %order_ref.7, s32[4,2]{1,0:T(4,128)} %copy.14.len_ref, bf16[128,8192]{1,0:T(8,128)(2,1)} %q_ref.7, bf16[128,512]{1,0:T(8,128)(2,1)} %refs_0_.7, ...), custom_call_target="tpu_custom_call" | custom-call | tf_op jit(solution)/shard_map/attend/pallas_call | solution.py:280
  24.0 2.4 %collective-permute-done.refs_2_.refs_3_ = bf16[128,768]{1,0:T(8,128)(2,1)S(1)} collective-permute-done((bf16[128,768]{1,0:T(8,128)(2,1)}, bf16[128,768]{1,0:T(8,128)(2,1)S(1)}, u32[]{:S(2)}, u32[]{:S(2)}) %collective-permute-start) | collective-permute-done | bytes 196640 | tf_op jit(solution)/shard_map/ppermute | solution.py:125
  27.5 8.9 %collective-permute-start.21 = (bf16[64,2048]{1,0:T(8,128)(2,1)}, bf16[64,2048]{1,0:T(8,128)(2,1)S(1)}, u32[]{:S(2)}, u32[]{:S(2)}) collective-permute-start(bf16[64,2048]{1,0:T(8,128)(2,1)} %get-tuple-element.54), channel_id=1, source_target_pairs={{0,14},{2,12},{4,10},{6,8},{8,22},{10,20},{12,18},{14,16},{16,30},... | collective-permute-start | bytes 786440 | tf_op jit(solution)/shard_map/ppermute | solution.py:135
  37.2 6.2 %attend.6 = (bf16[64,2048]{1,0:T(8,128)(2,1)}, bf16[64,2048]{1,0:T(8,128)(2,1)}, bf16[64,2048]{1,0:T(8,128)(2,1)}, bf16[64,2048]{1,0:T(8,128)(2,1)}) custom-call(s32[3]{0:T(128)} %pad_add_fusion.where_ref, s32[4,4]{1,0:T(4,128)} %order_ref.7, s32[4,2]{1,0:T(4,128)} %copy.14.len_ref, bf16[128,8192]{1,0:T(8,128)(2,1)} %q_ref.7, bf16[128,512]{1,0:T(8,128)(2,1)} %refs_0_.7, ...), custom_call_target="tpu_custom_call" | custom-call | tf_op jit(solution)/shard_map/attend/pallas_call | solution.py:280
  43.6 5.9 %collective-permute-start.15 = (bf16[64,2048]{1,0:T(8,128)(2,1)}, bf16[64,2048]{1,0:T(8,128)(2,1)S(1)}, u32[]{:S(2)}, u32[]{:S(2)}) collective-permute-start(bf16[64,2048]{1,0:T(8,128)(2,1)} %get-tuple-element.48), channel_id=1, source_target_pairs={{0,10},{2,8},{4,14},{6,12},{8,18},{10,16},{12,22},{14,20},{16,26},... | collective-permute-start | bytes 786440 | tf_op jit(solution)/shard_map/ppermute | solution.py:135
  49.4 6.2 %attend.5 = (bf16[64,2048]{1,0:T(8,128)(2,1)}, bf16[64,2048]{1,0:T(8,128)(2,1)}, bf16[64,2048]{1,0:T(8,128)(2,1)}, bf16[64,2048]{1,0:T(8,128)(2,1)}) custom-call(s32[3]{0:T(128)} %pad_add_fusion.where_ref, s32[4,4]{1,0:T(4,128)} %order_ref.7, s32[4,2]{1,0:T(4,128)} %copy.14.len_ref, bf16[128,8192]{1,0:T(8,128)(2,1)} %q_ref.7, bf16[128,512]{1,0:T(8,128)(2,1)} %refs_0_.7, ...), custom_call_target="tpu_custom_call" | custom-call | tf_op jit(solution)/shard_map/attend/pallas_call | solution.py:280
  56.3 2.3 %collective-permute-start.16 = (bf16[64,2048]{1,0:T(8,128)(2,1)}, bf16[64,2048]{1,0:T(8,128)(2,1)S(1)}, u32[]{:S(2)}, u32[]{:S(2)}) collective-permute-start(bf16[64,2048]{1,0:T(8,128)(2,1)} %get-tuple-element.49), channel_id=1, source_target_pairs={{0,12},{2,14},{4,8},{6,10},{8,20},{10,22},{12,16},{14,18},{16,28},... | collective-permute-start | bytes 786440 | tf_op jit(solution)/shard_map/ppermute | solution.py:135
  59.3 2.3 %collective-permute-start.17 = (bf16[64,2048]{1,0:T(8,128)(2,1)}, bf16[64,2048]{1,0:T(8,128)(2,1)S(1)}, u32[]{:S(2)}, u32[]{:S(2)}) collective-permute-start(bf16[64,2048]{1,0:T(8,128)(2,1)} %get-tuple-element.50), channel_id=1, source_target_pairs={{0,14},{2,12},{4,10},{6,8},{8,22},{10,20},{12,18},{14,16},{16,30},... | collective-permute-start | bytes 786440 | tf_op jit(solution)/shard_map/ppermute | solution.py:135
  62.6 6.8 %collective-permute-start.11 = (bf16[64,2048]{1,0:T(8,128)(2,1)}, bf16[64,2048]{1,0:T(8,128)(2,1)S(1)}, u32[]{:S(2)}, u32[]{:S(2)}) collective-permute-start(bf16[64,2048]{1,0:T(8,128)(2,1)} %get-tuple-element.44), channel_id=1, source_target_pairs={{0,10},{2,8},{4,14},{6,12},{8,18},{10,16},{12,22},{14,20},{16,26},... | collective-permute-start | bytes 786440 | tf_op jit(solution)/shard_map/ppermute | solution.py:135
  69.5 3.0 %collective-permute-start.12 = (bf16[64,2048]{1,0:T(8,128)(2,1)}, bf16[64,2048]{1,0:T(8,128)(2,1)S(1)}, u32[]{:S(2)}, u32[]{:S(2)}) collective-permute-start(bf16[64,2048]{1,0:T(8,128)(2,1)} %get-tuple-element.45), channel_id=1, source_target_pairs={{0,12},{2,14},{4,8},{6,10},{8,20},{10,22},{12,16},{14,18},{16,28},... | collective-permute-start | bytes 786440 | tf_op jit(solution)/shard_map/ppermute | solution.py:135
  72.4 6.2 %attend.4 = (bf16[64,2048]{1,0:T(8,128)(2,1)}, bf16[64,2048]{1,0:T(8,128)(2,1)}, bf16[64,2048]{1,0:T(8,128)(2,1)}, bf16[64,2048]{1,0:T(8,128)(2,1)}) custom-call(s32[3]{0:T(128)} %pad_add_fusion.where_ref, s32[4,4]{1,0:T(4,128)} %order_ref.7, s32[4,2]{1,0:T(4,128)} %copy.14.len_ref, bf16[128,8192]{1,0:T(8,128)(2,1)} %q_ref.7, bf16[128,512]{1,0:T(8,128)(2,1)} %refs_0_.7, ...), custom_call_target="tpu_custom_call" | custom-call | tf_op jit(solution)/shard_map/attend/pallas_call | solution.py:280
  80.7 10.8 %collective-permute-start.4 = (bf16[64,2048]{1,0:T(8,128)(2,1)}, bf16[64,2048]{1,0:T(8,128)(2,1)S(1)}, u32[]{:S(2)}, u32[]{:S(2)}) collective-permute-start(bf16[64,2048]{1,0:T(8,128)(2,1)} %get-tuple-element.37), channel_id=1, source_target_pairs={{0,10},{2,8},{4,14},{6,12},{8,18},{10,16},{12,22},{14,20},{16,26},... | collective-permute-start | bytes 786440 | tf_op jit(solution)/shard_map/ppermute | solution.py:135
  91.5 6.5 %collective-permute-start.5 = (bf16[64,2048]{1,0:T(8,128)(2,1)}, bf16[64,2048]{1,0:T(8,128)(2,1)S(1)}, u32[]{:S(2)}, u32[]{:S(2)}) collective-permute-start(bf16[64,2048]{1,0:T(8,128)(2,1)} %get-tuple-element.38), channel_id=1, source_target_pairs={{0,12},{2,14},{4,8},{6,10},{8,20},{10,22},{12,16},{14,18},{16,28},... | collective-permute-start | bytes 786440 | tf_op jit(solution)/shard_map/ppermute | solution.py:135
  97.9 3.9 %collective-permute-start.6 = (bf16[64,2048]{1,0:T(8,128)(2,1)}, bf16[64,2048]{1,0:T(8,128)(2,1)S(1)}, u32[]{:S(2)}, u32[]{:S(2)}) collective-permute-start(bf16[64,2048]{1,0:T(8,128)(2,1)} %get-tuple-element.39), channel_id=1, source_target_pairs={{0,14},{2,12},{4,10},{6,8},{8,22},{10,20},{12,18},{14,16},{16,30},... | collective-permute-start | bytes 786440 | tf_op jit(solution)/shard_map/ppermute | solution.py:135
  103.8 4.5 %unpack_rows.4 = (bf16[128,16384]{1,0:T(8,128)(2,1)}, bf16[128,2048]{1,0:T(8,128)(2,1)}) custom-call(s32[3]{0:T(128)} %pad_add_fusion.where_ref, bf16[64,2048]{1,0:T(8,128)(2,1)} %copy-done.22, bf16[64,2048]{1,0:T(8,128)(2,1)} %copy-done.23, bf16[64,2048]{1,0:T(8,128)(2,1)} %copy-done.24, bf16[64,2048]{1,0:T(8,128)(2,1)} %copy-done.25, ...), custom_call_target="tpu_custom_call" | custom-call | tf_op jit(solution)/shard_map/unpack_rows/pallas_call | solution.py:321
  108.3 4.4 %unpack_rows.5 = (bf16[128,16384]{1,0:T(8,128)(2,1)}, bf16[128,2048]{1,0:T(8,128)(2,1)}) custom-call(s32[3]{0:T(128)} %pad_add_fusion.where_ref, bf16[64,2048]{1,0:T(8,128)(2,1)} %copy-done.10, bf16[64,2048]{1,0:T(8,128)(2,1)} %copy-done.11, bf16[64,2048]{1,0:T(8,128)(2,1)} %copy-done.12, ...), custom_call_target="tpu_custom_call", output_to_operand_aliasing={{0}: (7, {})} | custom-call | tf_op jit(solution)/shard_map/unpack_rows/pallas_call | solution.py:321
  112.7 21.6 %collective-permute-start.25 = (bf16[128,2048]{1,0:T(8,128)(2,1)}, bf16[128,2048]{1,0:T(8,128)(2,1)S(1)}, u32[]{:S(2)}, u32[]{:S(2)}) collective-permute-start(bf16[128,2048]{1,0:T(8,128)(2,1)} %get-tuple-element.61), channel_id=1, source_target_pairs={{0,1},{1,0},{2,3},{3,2},{4,5},{5,4},{6,7},{7,6},{8,9},{9,8},{10,11... | collective-permute-start | bytes 1572872 | tf_op jit(solution)/shard_map/ppermute | solution.py:408
  134.3 4.4 %unpack_rows.6 = (bf16[128,16384]{1,0:T(8,128)(2,1)}, bf16[128,2048]{1,0:T(8,128)(2,1)}) custom-call(s32[3]{0:T(128)} %pad_add_fusion.where_ref, bf16[64,2048]{1,0:T(8,128)(2,1)} %copy-done.13, bf16[64,2048]{1,0:T(8,128)(2,1)} %copy-done.15, bf16[64,2048]{1,0:T(8,128)(2,1)} %copy-done.17, ...), custom_call_target="tpu_custom_call", output_to_operand_aliasing={{0}: (7, {})} | custom-call | tf_op jit(solution)/shard_map/unpack_rows/pallas_call | solution.py:321
  140.3 4.4 %unpack_rows.7 = (bf16[128,16384]{1,0:T(8,128)(2,1)}, bf16[128,2048]{1,0:T(8,128)(2,1)}) custom-call(s32[3]{0:T(128)} %pad_add_fusion.where_ref, bf16[64,2048]{1,0:T(8,128)(2,1)} %copy-done.16, bf16[64,2048]{1,0:T(8,128)(2,1)} %copy-done.18, bf16[64,2048]{1,0:T(8,128)(2,1)} %copy-done.19, ...), custom_call_target="tpu_custom_call", output_to_operand_aliasing={{0}: (7, {})} | custom-call | tf_op jit(solution)/shard_map/unpack_rows/pallas_call | solution.py:321
  146.0 3.8 %place_twin.4.old_ref = bf16[128,16384]{1,0:T(8,128)(2,1)} custom-call(s32[3]{0:T(128)} %pad_add_fusion.where_ref, bf16[128,2048]{1,0:T(8,128)(2,1)} %copy-done.6, bf16[128,16384]{1,0:T(8,128)(2,1)} %get-tuple-element.62.old_ref), custom_call_target="tpu_custom_call", output_to_operand_aliasing={{}: (2, {})} | custom-call | tf_op jit(solution)/shard_map/place_twin/pallas_call | solution.py:349
  150.6 3.8 %place_twin.5.old_ref = bf16[128,16384]{1,0:T(8,128)(2,1)} custom-call(s32[3]{0:T(128)} %pad_add_fusion.where_ref, bf16[128,2048]{1,0:T(8,128)(2,1)} %copy-done.7, bf16[128,16384]{1,0:T(8,128)(2,1)} %place_twin.4.old_ref), custom_call_target="tpu_custom_call", output_to_operand_aliasing={{}: (2, {})} | custom-call | tf_op jit(solution)/shard_map/place_twin/pallas_call | solution.py:349
  155.3 3.8 %place_twin.6.old_ref = bf16[128,16384]{1,0:T(8,128)(2,1)} custom-call(s32[3]{0:T(128)} %pad_add_fusion.where_ref, bf16[128,2048]{1,0:T(8,128)(2,1)} %copy-done.8, bf16[128,16384]{1,0:T(8,128)(2,1)} %place_twin.5.old_ref), custom_call_target="tpu_custom_call", output_to_operand_aliasing={{}: (2, {})} | custom-call | tf_op jit(solution)/shard_map/place_twin/pallas_call | solution.py:349
  159.9 3.8 %place_twin.7 = bf16[128,16384]{1,0:T(8,128)(2,1)} custom-call(s32[3]{0:T(128)} %pad_add_fusion.where_ref, bf16[128,2048]{1,0:T(8,128)(2,1)} %copy-done.9, bf16[128,16384]{1,0:T(8,128)(2,1)} %place_twin.6.old_ref), custom_call_target="tpu_custom_call", output_to_operand_aliasing={{}: (2, {})} | custom-call | tf_op jit(solution)/shard_map/place_twin/pallas_call | solution.py:349
  (96 shorter events, 28.9 us)
Async XLA Ops:
  6.0 5.2 %collective-permute-start.9 = (bf16[144,256]{1,0:T(8,128)(2,1)}, bf16[144,256]{1,0:T(8,128)(2,1)S(1)}, u32[]{:S(2)}, u32[]{:S(2)}) collective-permute-start(bf16[144,256]{1,0:T(8,128)(2,1)} %get-tuple-element.40), channel_id=1, source_target_pairs={{0,6},{2,4},{4,2},{6,0},{1,7},{3,5},{5,3},{7,1},{8,14},{10,12},{12... | collective-permute-start | bytes 221192 | tf_op jit(solution)/shard_map/ppermute | solution.py:125
  17.9 25.7 %collective-permute-start.18 = (bf16[64,2048]{1,0:T(8,128)(2,1)}, bf16[64,2048]{1,0:T(8,128)(2,1)S(1)}, u32[]{:S(2)}, u32[]{:S(2)}) collective-permute-start(bf16[64,2048]{1,0:T(8,128)(2,1)} %get-tuple-element.51), channel_id=1, source_target_pairs={{0,8},{2,10},{4,12},{6,14},{8,16},{10,18},{12,20},{14,22},{16,24},... | collective-permute-start | bytes 786440 | tf_op jit(solution)/shard_map/ppermute | solution.py:135
  19.1 7.2 %collective-permute-start = (bf16[128,768]{1,0:T(8,128)(2,1)}, bf16[128,768]{1,0:T(8,128)(2,1)S(1)}, u32[]{:S(2)}, u32[]{:S(2)}) collective-permute-start(bf16[128,768]{1,0:T(8,128)(2,1)} %get-tuple-element.34), channel_id=1, source_target_pairs={{0,2},{2,0},{4,6},{6,4},{1,3},{3,1},{5,7},{7,5},{8,10},{10,8},{12,... | collective-permute-start | bytes 589832 | tf_op jit(solution)/shard_map/ppermute | solution.py:125
  20.1 7.5 %collective-permute-start.1 = (bf16[128,768]{1,0:T(8,128)(2,1)}, bf16[128,768]{1,0:T(8,128)(2,1)S(1)}, u32[]{:S(2)}, u32[]{:S(2)}) collective-permute-start(bf16[128,768]{1,0:T(8,128)(2,1)} %get-tuple-element.34), channel_id=1, source_target_pairs={{0,4},{2,6},{4,0},{6,2},{1,5},{3,7},{5,1},{7,3},{8,12},{10,14},{12... | collective-permute-start | bytes 589832 | tf_op jit(solution)/shard_map/ppermute | solution.py:125
  21.6 14.9 %collective-permute-start.2 = (bf16[128,768]{1,0:T(8,128)(2,1)}, bf16[128,768]{1,0:T(8,128)(2,1)S(1)}, u32[]{:S(2)}, u32[]{:S(2)}) collective-permute-start(bf16[128,768]{1,0:T(8,128)(2,1)} %get-tuple-element.34), channel_id=1, source_target_pairs={{0,6},{2,4},{4,2},{6,0},{1,7},{3,5},{5,3},{7,1},{8,14},{10,12},{12... | collective-permute-start | bytes 589832 | tf_op jit(solution)/shard_map/ppermute | solution.py:125
  22.8 32.8 %collective-permute-start.19 = (bf16[64,2048]{1,0:T(8,128)(2,1)}, bf16[64,2048]{1,0:T(8,128)(2,1)S(1)}, u32[]{:S(2)}, u32[]{:S(2)}) collective-permute-start(bf16[64,2048]{1,0:T(8,128)(2,1)} %get-tuple-element.52), channel_id=1, source_target_pairs={{0,10},{2,8},{4,14},{6,12},{8,18},{10,16},{12,22},{14,20},{16,26},... | collective-permute-start | bytes 786440 | tf_op jit(solution)/shard_map/ppermute | solution.py:135
  26.4 32.2 %collective-permute-start.20 = (bf16[64,2048]{1,0:T(8,128)(2,1)}, bf16[64,2048]{1,0:T(8,128)(2,1)S(1)}, u32[]{:S(2)}, u32[]{:S(2)}) collective-permute-start(bf16[64,2048]{1,0:T(8,128)(2,1)} %get-tuple-element.53), channel_id=1, source_target_pairs={{0,12},{2,14},{4,8},{6,10},{8,20},{10,22},{12,16},{14,18},{16,28},... | collective-permute-start | bytes 786440 | tf_op jit(solution)/shard_map/ppermute | solution.py:135
  27.5 34.1 %collective-permute-start.21 = (bf16[64,2048]{1,0:T(8,128)(2,1)}, bf16[64,2048]{1,0:T(8,128)(2,1)S(1)}, u32[]{:S(2)}, u32[]{:S(2)}) collective-permute-start(bf16[64,2048]{1,0:T(8,128)(2,1)} %get-tuple-element.54), channel_id=1, source_target_pairs={{0,14},{2,12},{4,10},{6,8},{8,22},{10,20},{12,18},{14,16},{16,30},... | collective-permute-start | bytes 786440 | tf_op jit(solution)/shard_map/ppermute | solution.py:135
  43.4 19.3 %collective-permute-start.14 = (bf16[64,2048]{1,0:T(8,128)(2,1)}, bf16[64,2048]{1,0:T(8,128)(2,1)S(1)}, u32[]{:S(2)}, u32[]{:S(2)}) collective-permute-start(bf16[64,2048]{1,0:T(8,128)(2,1)} %get-tuple-element.47), channel_id=1, source_target_pairs={{0,8},{2,10},{4,12},{6,14},{8,16},{10,18},{12,20},{14,22},{16,24},... | collective-permute-start | bytes 786440 | tf_op jit(solution)/shard_map/ppermute | solution.py:135
  43.6 25.9 %collective-permute-start.15 = (bf16[64,2048]{1,0:T(8,128)(2,1)}, bf16[64,2048]{1,0:T(8,128)(2,1)S(1)}, u32[]{:S(2)}, u32[]{:S(2)}) collective-permute-start(bf16[64,2048]{1,0:T(8,128)(2,1)} %get-tuple-element.48), channel_id=1, source_target_pairs={{0,10},{2,8},{4,14},{6,12},{8,18},{10,16},{12,22},{14,20},{16,26},... | collective-permute-start | bytes 786440 | tf_op jit(solution)/shard_map/ppermute | solution.py:135
  56.3 22.4 %collective-permute-start.16 = (bf16[64,2048]{1,0:T(8,128)(2,1)}, bf16[64,2048]{1,0:T(8,128)(2,1)S(1)}, u32[]{:S(2)}, u32[]{:S(2)}) collective-permute-start(bf16[64,2048]{1,0:T(8,128)(2,1)} %get-tuple-element.49), channel_id=1, source_target_pairs={{0,12},{2,14},{4,8},{6,10},{8,20},{10,22},{12,16},{14,18},{16,28},... | collective-permute-start | bytes 786440 | tf_op jit(solution)/shard_map/ppermute | solution.py:135
  59.3 20.9 %collective-permute-start.17 = (bf16[64,2048]{1,0:T(8,128)(2,1)}, bf16[64,2048]{1,0:T(8,128)(2,1)S(1)}, u32[]{:S(2)}, u32[]{:S(2)}) collective-permute-start(bf16[64,2048]{1,0:T(8,128)(2,1)} %get-tuple-element.50), channel_id=1, source_target_pairs={{0,14},{2,12},{4,10},{6,8},{8,22},{10,20},{12,18},{14,16},{16,30},... | collective-permute-start | bytes 786440 | tf_op jit(solution)/shard_map/ppermute | solution.py:135
  61.7 19.0 %collective-permute-start.10 = (bf16[64,2048]{1,0:T(8,128)(2,1)}, bf16[64,2048]{1,0:T(8,128)(2,1)S(1)}, u32[]{:S(2)}, u32[]{:S(2)}) collective-permute-start(bf16[64,2048]{1,0:T(8,128)(2,1)} %get-tuple-element.43), channel_id=1, source_target_pairs={{0,8},{2,10},{4,12},{6,14},{8,16},{10,18},{12,20},{14,22},{16,24},... | collective-permute-start | bytes 786440 | tf_op jit(solution)/shard_map/ppermute | solution.py:135
  62.6 28.8 %collective-permute-start.11 = (bf16[64,2048]{1,0:T(8,128)(2,1)}, bf16[64,2048]{1,0:T(8,128)(2,1)S(1)}, u32[]{:S(2)}, u32[]{:S(2)}) collective-permute-start(bf16[64,2048]{1,0:T(8,128)(2,1)} %get-tuple-element.44), channel_id=1, source_target_pairs={{0,10},{2,8},{4,14},{6,12},{8,18},{10,16},{12,22},{14,20},{16,26},... | collective-permute-start | bytes 786440 | tf_op jit(solution)/shard_map/ppermute | solution.py:135
  69.5 28.5 %collective-permute-start.12 = (bf16[64,2048]{1,0:T(8,128)(2,1)}, bf16[64,2048]{1,0:T(8,128)(2,1)S(1)}, u32[]{:S(2)}, u32[]{:S(2)}) collective-permute-start(bf16[64,2048]{1,0:T(8,128)(2,1)} %get-tuple-element.45), channel_id=1, source_target_pairs={{0,12},{2,14},{4,8},{6,10},{8,20},{10,22},{12,16},{14,18},{16,28},... | collective-permute-start | bytes 786440 | tf_op jit(solution)/shard_map/ppermute | solution.py:135
  78.7 34.1 %collective-permute-start.13 = (bf16[64,2048]{1,0:T(8,128)(2,1)}, bf16[64,2048]{1,0:T(8,128)(2,1)S(1)}, u32[]{:S(2)}, u32[]{:S(2)}) collective-permute-start(bf16[64,2048]{1,0:T(8,128)(2,1)} %get-tuple-element.46), channel_id=1, source_target_pairs={{0,14},{2,12},{4,10},{6,8},{8,22},{10,20},{12,18},{14,16},{16,30},... | collective-permute-start | bytes 786440 | tf_op jit(solution)/shard_map/ppermute | solution.py:135
  80.2 58.5 %collective-permute-start.3 = (bf16[64,2048]{1,0:T(8,128)(2,1)}, bf16[64,2048]{1,0:T(8,128)(2,1)S(1)}, u32[]{:S(2)}, u32[]{:S(2)}) collective-permute-start(bf16[64,2048]{1,0:T(8,128)(2,1)} %get-tuple-element.36), channel_id=1, source_target_pairs={{0,8},{2,10},{4,12},{6,14},{8,16},{10,18},{12,20},{14,22},{16,24},... | collective-permute-start | bytes 786440 | tf_op jit(solution)/shard_map/ppermute | solution.py:135
  80.7 58.8 %collective-permute-start.4 = (bf16[64,2048]{1,0:T(8,128)(2,1)}, bf16[64,2048]{1,0:T(8,128)(2,1)S(1)}, u32[]{:S(2)}, u32[]{:S(2)}) collective-permute-start(bf16[64,2048]{1,0:T(8,128)(2,1)} %get-tuple-element.37), channel_id=1, source_target_pairs={{0,10},{2,8},{4,14},{6,12},{8,18},{10,16},{12,22},{14,20},{16,26},... | collective-permute-start | bytes 786440 | tf_op jit(solution)/shard_map/ppermute | solution.py:135
  91.5 48.1 %collective-permute-start.5 = (bf16[64,2048]{1,0:T(8,128)(2,1)}, bf16[64,2048]{1,0:T(8,128)(2,1)S(1)}, u32[]{:S(2)}, u32[]{:S(2)}) collective-permute-start(bf16[64,2048]{1,0:T(8,128)(2,1)} %get-tuple-element.38), channel_id=1, source_target_pairs={{0,12},{2,14},{4,8},{6,10},{8,20},{10,22},{12,16},{14,18},{16,28},... | collective-permute-start | bytes 786440 | tf_op jit(solution)/shard_map/ppermute | solution.py:135
  97.9 41.6 %collective-permute-start.6 = (bf16[64,2048]{1,0:T(8,128)(2,1)}, bf16[64,2048]{1,0:T(8,128)(2,1)S(1)}, u32[]{:S(2)}, u32[]{:S(2)}) collective-permute-start(bf16[64,2048]{1,0:T(8,128)(2,1)} %get-tuple-element.39), channel_id=1, source_target_pairs={{0,14},{2,12},{4,10},{6,8},{8,22},{10,20},{12,18},{14,16},{16,30},... | collective-permute-start | bytes 786440 | tf_op jit(solution)/shard_map/ppermute | solution.py:135
  112.7 32.4 %collective-permute-start.25 = (bf16[128,2048]{1,0:T(8,128)(2,1)}, bf16[128,2048]{1,0:T(8,128)(2,1)S(1)}, u32[]{:S(2)}, u32[]{:S(2)}) collective-permute-start(bf16[128,2048]{1,0:T(8,128)(2,1)} %get-tuple-element.61), channel_id=1, source_target_pairs={{0,1},{1,0},{2,3},{3,2},{4,5},{5,4},{6,7},{7,6},{8,9},{9,8},{10,11... | collective-permute-start | bytes 1572872 | tf_op jit(solution)/shard_map/ppermute | solution.py:408
  138.8 11.0 %collective-permute-start.24 = (bf16[128,2048]{1,0:T(8,128)(2,1)}, bf16[128,2048]{1,0:T(8,128)(2,1)S(1)}, u32[]{:S(2)}, u32[]{:S(2)}) collective-permute-start(bf16[128,2048]{1,0:T(8,128)(2,1)} %get-tuple-element.60), channel_id=1, source_target_pairs={{0,1},{1,0},{2,3},{3,2},{4,5},{5,4},{6,7},{7,6},{8,9},{9,8},{10,11... | collective-permute-start | bytes 1572872 | tf_op jit(solution)/shard_map/ppermute | solution.py:408
  139.4 15.0 %collective-permute-start.23 = (bf16[128,2048]{1,0:T(8,128)(2,1)}, bf16[128,2048]{1,0:T(8,128)(2,1)S(1)}, u32[]{:S(2)}, u32[]{:S(2)}) collective-permute-start(bf16[128,2048]{1,0:T(8,128)(2,1)} %get-tuple-element.59), channel_id=1, source_target_pairs={{0,1},{1,0},{2,3},{3,2},{4,5},{5,4},{6,7},{7,6},{8,9},{9,8},{10,11... | collective-permute-start | bytes 1572872 | tf_op jit(solution)/shard_map/ppermute | solution.py:408
  144.7 14.3 %collective-permute-start.22 = (bf16[128,2048]{1,0:T(8,128)(2,1)}, bf16[128,2048]{1,0:T(8,128)(2,1)S(1)}, u32[]{:S(2)}, u32[]{:S(2)}) collective-permute-start(bf16[128,2048]{1,0:T(8,128)(2,1)} %get-tuple-element.58), channel_id=1, source_target_pairs={{0,1},{1,0},{2,3},{3,2},{4,5},{5,4},{6,7},{7,6},{8,9},{9,8},{10,11... | collective-permute-start | bytes 1572872 | tf_op jit(solution)/shard_map/ppermute | solution.py:408
  (28 other events, 402.3 us)

commit v2 on v0

--- a/solution.py
+++ b/solution.py
@@ -1,6 +1,8 @@
 import jax
 import jax.numpy as jnp
 from jax import lax
+from jax.experimental import pallas as pl
+from jax.experimental.pallas import tpu as pltpu
 from jax.sharding import PartitionSpec as P
 
 HD = 128
@@ -54,7 +56,7 @@
     return spread_rows(buffer, cycle_size, split_size, capacity, width)
 
 
-def body(queries, keys, values, pair_order, lengths, routes):
+def general_body(queries, keys, values, pair_order, lengths, routes):
     cycle_size = lax.axis_size("cp")
     split_size = lax.axis_size("tp")
     section = lax.axis_index("pp")
@@ -118,6 +120,325 @@
     return shifted(arranged, "pp", 1)
 
 
+def to_partner(block, mask):
+    size = lax.axis_size("cp")
+    return lax.ppermute(block, "cp", [(i, i ^ mask) for i in range(size)])
+
+
+def to_next_section(block, mask):
+    sections, size = lax.axis_size("pp"), lax.axis_size("cp")
+    route = [
+        (p * size + i, ((p + 1) % sections) * size + (i ^ mask))
+        for p in range(sections)
+        for i in range(size)
+    ]
+    return lax.ppermute(block, ("pp", "cp"), route)
+
+
+def row_to_column(row):
+    count = row.shape[1]
+    down = lax.broadcasted_iota(jnp.int32, (count, count), 0)
+    across = lax.broadcasted_iota(jnp.int32, (count, count), 1)
+    return jnp.sum(jnp.where(down == across, row, 0), axis=1, keepdims=True)
+
+
+def rank_in_row(row):
+    count = row.shape[1]
+    down = lax.broadcasted_iota(jnp.int32, (count, count), 0)
+    across = lax.broadcasted_iota(jnp.int32, (count, count), 1)
+    hits = jnp.logical_and(row_to_column(row) == row, down < across)
+    return jnp.sum(hits.astype(jnp.int32), axis=0, keepdims=True)
+
+
+def one_hot(rank, match, height):
+    ids = lax.broadcasted_iota(jnp.int32, (height, rank.shape[1]), 0)
+    return jnp.logical_and(ids == rank, match).astype(jnp.float32).astype(jnp.bfloat16)
+
+
+def in_vmem(array):
+    return pltpu.with_memory_space_constraint(array, pltpu.VMEM)
+
+
+def specs(space, count):
+    return [pl.BlockSpec(memory_space=space)] * count
+
+
+def make_ready(keys, values, pair_order, limits, route_rows, where, *, cycle_size, split_size, packed_rows):
+    row_count, width = keys.shape
+    sections = route_rows.shape[0]
+    half = row_count // 2
+    block_len = half // 2
+    head_rows = row_count + 16
+    total = cycle_size * packed_rows
+
+    def kernel(where_ref, order_ref, limit_ref, k_ref, v_ref, r_ref, first_ref, rest_ref, pack_ref, mask_ref):
+        section, place = where_ref[0], where_ref[1]
+        first_ref[0:row_count, 0:HD] = k_ref[:, 0:HD]
+        first_ref[0:row_count, HD : 2 * HD] = v_ref[:, 0:HD]
+        spare = jnp.zeros((16 - sections, row_count), jnp.float32)
+        sent = jnp.concatenate([r_ref[...].astype(jnp.float32), spare], axis=0).astype(jnp.bfloat16)
+        first_ref[row_count:head_rows, 0:HD] = sent
+        first_ref[row_count:head_rows, HD : 2 * HD] = jnp.zeros((16, HD), jnp.bfloat16)
+        rest_ref[:, 0 : width - HD] = k_ref[:, HD:width]
+        rest_ref[:, width - HD :] = v_ref[:, HD:width]
+        chips = r_ref[pl.ds(section, 1), :] // split_size
+        rank = rank_in_row(chips)
+        none = jnp.zeros((packed_rows, half), jnp.float32)
+        for mask in range(cycle_size):
+            ids = lax.broadcasted_iota(jnp.int32, (packed_rows, row_count), 0)
+            pick = jnp.logical_and(ids == rank, chips == (place ^ mask)).astype(jnp.float32)
+            first, second = pick[:, :half], pick[:, half:]
+            rows = slice(mask * packed_rows, (mask + 1) * packed_rows)
+            later = slice(total + mask * packed_rows, total + (mask + 1) * packed_rows)
+            pack_ref[rows, :] = jnp.concatenate([first, none, second, none], axis=1).astype(jnp.bfloat16)
+            pack_ref[later, :] = jnp.concatenate([none, first, none, second], axis=1).astype(jnp.bfloat16)
+        own = order_ref[section, place]
+        lane = lax.broadcasted_iota(jnp.int32, (half, 2 * half), 1) % half
+        query_pos = jnp.where(lane < block_len, own, 2 * cycle_size - 2 - own) * block_len + lane
+        down = lax.broadcasted_iota(jnp.int32, (half, 2 * half), 0)
+        for mask in range(cycle_size):
+            pair = order_ref[section, place ^ mask]
+            key_pos = jnp.where(down < block_len, pair, 2 * cycle_size - 2 - pair) * block_len + down
+            for seq in range(2):
+                allowed = jnp.logical_and(key_pos <= query_pos, key_pos < limit_ref[seq, section])
+                mask_ref[seq, mask * half : (mask + 1) * half, :] = allowed.astype(jnp.float32)
+
+    return pl.pallas_call(
+        kernel,
+        out_shape=(
+            pltpu.VMEM((head_rows, 2 * HD), jnp.bfloat16),
+            pltpu.VMEM((row_count, 2 * (width - HD)), jnp.bfloat16),
+            pltpu.VMEM((2 * total, 2 * row_count), jnp.bfloat16),
+            pltpu.VMEM((2, cycle_size * half, row_count), jnp.float32),
+        ),
+        in_specs=specs(pltpu.SMEM, 3) + specs(pltpu.VMEM, 3),
+        out_specs=tuple(specs(pltpu.VMEM, 4)),
+        name="make_ready",
+    )(where, pair_order, limits, keys, values, route_rows)
+
+
+def make_unpack(route_rows, heads, where, *, cycle_size, split_size, packed_rows, capacity):
+    sections, row_count = route_rows.shape
+    slot_rows = cycle_size * capacity
+
+    def kernel(where_ref, r_ref, *refs):
+        head_refs, slots_ref = refs[: cycle_size - 1], refs[cycle_size - 1]
+        place, core = where_ref[1], where_ref[2]
+        source = (where_ref[0] + sections - 1) % sections
+        slots_ref[...] = jnp.zeros(slots_ref.shape, jnp.bfloat16)
+        for mask in range(cycle_size):
+            if mask == 0:
+                targets = r_ref[pl.ds(source, 1), :]
+            else:
+                block = head_refs[mask - 1][row_count : row_count + 16, 0:row_count].astype(jnp.float32)
+                ids = lax.broadcasted_iota(jnp.int32, block.shape, 0)
+                targets = jnp.sum(jnp.where(ids == source, block, 0.0), axis=0, keepdims=True)
+                targets = targets.astype(jnp.int32)
+            chips = targets // split_size
+            packed = one_hot(rank_in_row(chips), chips == place, packed_rows)
+            slots = rank_in_row(targets)
+            for step, which in enumerate((core, 1 - core)):
+                slotted = one_hot(slots, targets == place * split_size + which, capacity)
+                at = pl.ds(pl.multiple_of(step * slot_rows + (place ^ mask) * capacity, capacity), capacity)
+                slots_ref[at, mask * packed_rows : (mask + 1) * packed_rows] = lax.dot_general(
+                    slotted, packed, (((1,), (1,)), ((), ())), preferred_element_type=jnp.float32
+                ).astype(jnp.bfloat16)
+
+    return pl.pallas_call(
+        kernel,
+        out_shape=pltpu.VMEM((split_size * slot_rows, cycle_size * packed_rows), jnp.bfloat16),
+        in_specs=specs(pltpu.SMEM, 1) + specs(pltpu.VMEM, cycle_size),
+        out_specs=specs(pltpu.VMEM, 1)[0],
+        name="make_unpack",
+    )(where, route_rows, *[in_vmem(head) for head in heads])
+
+
+def attend(queries, pieces, pack, allow, group, *, cycle_size, group_size, packed_rows):
+    row_count = queries.shape[0]
+    half = row_count // 2
+    total_rows = cycle_size * packed_rows
+    width = group_size * HD
+    step_heads = min(4, group_size)
+    step_width = step_heads * HD
+    steps = group_size // step_heads
+    scale = HD ** (-0.5)
+
+    def kernel(q_hbm, pack_ref, allow_ref, *refs):
+        kv_refs, out_refs = refs[:cycle_size], refs[cycle_size : 2 * cycle_size]
+        q_ref, sems = refs[2 * cycle_size :]
+        loads = []
+        for step in range(steps):
+            at = group * width + step * step_width
+            loads.append(
+                pltpu.make_async_copy(q_hbm.at[:, at : at + step_width], q_ref.at[step], sems.at[step])
+            )
+            loads[-1].start()
+
+        def stacked(kind, rows):
+            return jnp.concatenate(
+                [ref[rows, piece[kind] : piece[kind] + HD] for ref, piece in zip(kv_refs, pieces)], axis=0
+            )
+
+        seq_rows = [slice(seq * half, (seq + 1) * half) for seq in range(2)]
+        keys = [stacked(1, rows) for rows in seq_rows]
+        values = [stacked(2, rows) for rows in seq_rows]
+        for step in range(steps):
+            loads[step].wait()
+            attended = []
+            for seq in range(2):
+                q = jnp.concatenate(
+                    [q_ref[step, seq_rows[seq], h * HD : (h + 1) * HD] for h in range(step_heads)], axis=0
+                )
+                scores = lax.dot_general(
+                    keys[seq], q, (((1,), (1,)), ((), ())), preferred_element_type=jnp.float32
+                )
+                tiles, totals = [], []
+                for pair in range(step_heads // 2):
+                    block = scores[:, pair * 2 * half : (pair + 1) * 2 * half] * scale
+                    block = jnp.where(allow_ref[seq] > 0.0, block, masked_score)
+                    block = jnp.exp(block - jnp.max(block, axis=0, keepdims=True))
+                    totals.append(jnp.sum(block, axis=0, keepdims=True))
+                    tiles.append(block.astype(jnp.bfloat16))
+                weights = jnp.concatenate(tiles, axis=1)
+                total = jnp.concatenate(totals, axis=1)
+                summed = lax.dot_general(
+                    values[seq], weights, (((0,), (0,)), ((), ())), preferred_element_type=jnp.float32
+                )
+                attended.append((summed / total).astype(jnp.bfloat16))
+            for pair in range(step_heads // 2):
+                cols = slice(pair * 2 * half, (pair + 1) * 2 * half)
+                both = jnp.concatenate([attended[0][:, cols], attended[1][:, cols]], axis=1)
+                packed = lax.dot_general(
+                    pack_ref[...], both, (((1,), (1,)), ((), ())), preferred_element_type=jnp.float32
+                ).astype(jnp.bfloat16)
+                for which in range(2):
+                    head = step * step_heads + 2 * pair + which
+                    for mask in range(cycle_size):
+                        at = which * total_rows + mask * packed_rows
+                        out_refs[mask][:, head * HD : (head + 1) * HD] = packed[at : at + packed_rows]
+
+    return pl.pallas_call(
+        kernel,
+        in_specs=specs(pl.ANY, 1) + specs(pltpu.VMEM, 2 + cycle_size),
+        out_specs=specs(pltpu.VMEM, cycle_size),
+        out_shape=[pltpu.VMEM((packed_rows, width), jnp.bfloat16)] * cycle_size,
+        scratch_shapes=[
+            pltpu.VMEM((steps, row_count, step_width), jnp.bfloat16),
+            pltpu.SemaphoreType.DMA((steps,)),
+        ],
+        compiler_params=pltpu.CompilerParams(vmem_limit_bytes=32 * 1024 * 1024),
+        name="attend",
+    )(queries, in_vmem(pack), in_vmem(allow), *[in_vmem(piece[0]) for piece in pieces])
+
+
+def unpack_rows(received, slots, where, out, group, *, group_count):
+    cycle_size = len(received)
+    packed_rows, width = received[0].shape
+    rows = slots.shape[0] // 2
+    full = 2 * group_count * width
+    tile = 512
+
+    def kernel(where_ref, *refs):
+        in_refs, slots_ref = refs[:cycle_size], refs[cycle_size]
+        out_ref, send_ref, own_ref, sems = refs[-4:]
+        copies = []
+        for step, start in enumerate(range(0, width, tile)):
+            cols = slice(start, start + tile)
+            block = jnp.concatenate([ref[:, cols] for ref in in_refs], axis=0)
+            placed = jnp.dot(slots_ref[...], block, preferred_element_type=jnp.float32).astype(jnp.bfloat16)
+            own_ref[:, cols] = placed[:rows]
+            send_ref[:, cols] = placed[rows:]
+            at = (where_ref[2] * group_count + group) * width + start
+            at = pl.ds(pl.multiple_of(at, tile), tile)
+            copies.append(pltpu.make_async_copy(own_ref.at[:, cols], out_ref.at[:, at], sems.at[step]))
+            copies[-1].start()
+        for copy in copies:
+            copy.wait()
+
+    in_specs = specs(pltpu.SMEM, 1) + specs(pltpu.VMEM, cycle_size + 1)
+    args = [in_vmem(block) for block in received] + [in_vmem(slots)]
+    aliases = {}
+    if out is not None:
+        in_specs += specs(pl.ANY, 1)
+        aliases = {len(args) + 1: 0}
+        args.append(out)
+    return pl.pallas_call(
+        kernel,
+        in_specs=in_specs,
+        out_specs=specs(pl.ANY, 1) + specs(pltpu.VMEM, 1),
+        scratch_shapes=[pltpu.VMEM((rows, width), jnp.bfloat16), pltpu.SemaphoreType.DMA((width // tile,))],
+        out_shape=[jax.ShapeDtypeStruct((rows, full), jnp.bfloat16), pltpu.VMEM((rows, width), jnp.bfloat16)],
+        input_output_aliases=aliases,
+        name="unpack_rows",
+    )(where, *args)
+
+
+def place_twins(blocks, out, where):
+    count = len(blocks)
+    width = blocks[0].shape[1]
+
+    def kernel(where_ref, *refs):
+        in_refs, out_ref, sems = refs[:count], refs[-2], refs[-1]
+        copies = []
+        for group in range(count):
+            at = pl.multiple_of(((1 - where_ref[2]) * count + group) * width, width)
+            copies.append(
+                pltpu.make_async_copy(in_refs[group], out_ref.at[:, pl.ds(at, width)], sems.at[group])
+            )
+            copies[-1].start()
+        for copy in copies:
+            copy.wait()
+
+    return pl.pallas_call(
+        kernel,
+        in_specs=specs(pltpu.SMEM, 1) + specs(pltpu.VMEM, count) + specs(pl.ANY, 1),
+        out_specs=specs(pl.ANY, 1)[0],
+        scratch_shapes=[pltpu.SemaphoreType.DMA((count,))],
+        out_shape=jax.ShapeDtypeStruct(out.shape, out.dtype),
+        input_output_aliases={count + 1: 0},
+        name="place_twins",
+    )(where, *[in_vmem(block) for block in blocks], out)
+
+
+def body(queries, keys, values, pair_order, lengths, routes):
+    cycle_size = lax.axis_size("cp")
+    split_size = lax.axis_size("tp")
+    row_count, width = queries.shape
+    group_count = keys.shape[1] // HD
+    group_size = width // keys.shape[1]
+    dest_count = cycle_size * split_size
+    capacity = 2 * row_count // dest_count
+    packed_rows = min(row_count, split_size * capacity)
+    masks = [2, 3, 1, 0]
+    where = jnp.stack([lax.axis_index("pp"), lax.axis_index("cp"), lax.axis_index("tp")]).astype(jnp.int32)
+    route_rows = routes[:, :, 0]
+    sizes = dict(cycle_size=cycle_size, split_size=split_size, packed_rows=packed_rows)
+    head, rest, pack, allow = make_ready(keys, values, pair_order, lengths.T, route_rows, where, **sizes)
+    heads = {mask: to_partner(head, mask) for mask in masks if mask}
+    rests = {mask: to_partner(rest, mask) for mask in (2, 1)}
+    heads, rests = lax.optimization_barrier((heads, rests))
+    rests[3] = to_partner(rests[2], 1)
+    slots = make_unpack(route_rows, [heads[mask] for mask in range(1, cycle_size)], where, capacity=capacity, **sizes)
+    heads[0], rests[0] = head, rest
+    arrived = []
+    for group in range(group_count):
+        first = (group - 1) * HD
+        if group == 0:
+            pieces = [(heads[mask], 0, HD) for mask in range(cycle_size)]
+        else:
+            pieces = [(rests[mask], first, first + keys.shape[1] - HD) for mask in range(cycle_size)]
+        packed = attend(
+            queries, pieces, pack, allow, group, cycle_size=cycle_size, group_size=group_size, packed_rows=packed_rows
+        )
+        sent = {mask: to_next_section(packed[mask], mask) for mask in masks}
+        arrived.append([sent[mask] for mask in range(cycle_size)])
+    out, twins = None, []
+    for group in range(group_count):
+        out, send = unpack_rows(arrived[group], slots, where, out, group, group_count=group_count)
+        twins.append(lax.ppermute(send, "tp", [(0, 1), (1, 0)]))
+    return place_twins(twins, out, where)
+
+
 def solution(mesh):
     placed = (
         P(("pp", "cp"), "tp"),
@@ -127,6 +448,11 @@
         P(),
         P(None, "cp", None),
     )
+    small = mesh.shape["cp"] == 4 and mesh.shape["tp"] == 2
     return jax.shard_map(
-        body, mesh=mesh, in_specs=placed, out_specs=P(("pp", "cp", "tp"), None), check_vma=False
+        body if small else general_body,
+        mesh=mesh,
+        in_specs=placed,
+        out_specs=P(("pp", "cp", "tp"), None),
+        check_vma=False,
     )

time: 288 us -> 137 us (0.48)
  blocking collectives: 131 us -> 0 us
  starting transfers between devices: 1.55 us -> 56.7 us
  waiting for transfers between devices: 91.3 us -> 39.1 us
  local copies, waits for them, and re-layouts: 42 us -> 6.84 us
  Pallas kernels: 0 us -> 33.3 us
  matrix products: 12.6 us -> 0 us
  other arithmetic: 6.85 us -> 0.65 us
    all_to_all x1 -> x0, blocking collectives: 97.9 us -> none  [spread_rows(): lax.all_to_all(flat_buffer, ('cp', 'tp'), split_axis=0, concat_axis=0, ti...]
    ppermute x1 -> x26, starting transfers between devices: 1.55 us -> 56.7 us  [the longest x16 44.1 us: to_next_section(): return lax.ppermute(block, ('pp', 'cp'), route)]
    ppermute x1 -> x26, waiting for transfers between devices: 91.3 us -> 39.1 us  [the longest x16 23.7 us: to_next_section(): return lax.ppermute(block, ('pp', 'cp'), route)]
    all_gather x2 -> x0, blocking collectives: 33.6 us -> none  [the longest x1 17.4 us: body(): key_piece = lax.all_gather(keys, 'cp', axis=0, tiled=True)]
    pallas_call x0 -> x11, Pallas kernels: none -> 33.3 us  [the longest x4 18 us: attend(): pl.pallas_call(kernel, in_specs=specs(pl.ANY, 1) + specs(pltpu.VMEM, 2 +...]
    convert_element_type x2 -> x0, local copies, waits for them, and re-layouts: 19.2 us -> none  [the longest x1 17.2 us: body(): weights.astype(jnp.bfloat16).reshape(stat_shape + (block, 2 * block_len))]
    dot_general x4 -> x0, matrix products: 12.6 us -> none  [the longest x1 5.7 us: body(): jnp.einsum('sqgrnk,nskgd->sqgrd', shaped, value_block, preferred_element_...]
    reshape x4 -> x0, local copies, waits for them, and re-layouts: 9.45 us -> none  [the longest x1 6.38 us: spread_rows(): moved.reshape(cycle_size, split_size, capacity, width)]
  transfers between devices with their start and end apart: 1 -> 26, of which waited for: 1 -> 8; matrix products, arithmetic and copies ran while one was open for 0% -> 0% of each run, Pallas kernels for 0% -> 19%
where the time goes in v2:
time: 137 us
  starting transfers between devices  56.7 us (41%)
  waiting for transfers between devices  39.1 us (29%)
  Pallas kernels  33.3 us (24%)
  local copies, waits for them, and re-layouts  6.84 us (5%)
    ppermute x16, starting transfers between devices, to_next_section(): return lax.ppermute(block, ('pp', 'cp'), route)  44.1 us
    ppermute x16, waiting for transfers between devices, to_next_section(): return lax.ppermute(block, ('pp', 'cp'), route)  23.7 us
    pallas_call x4, Pallas kernels, attend(): pl.pallas_call(kernel, in_specs=specs(pl.ANY, 1) + specs(pltpu.VMEM, 2 +...  18 us
    ppermute x6, waiting for transfers between devices, to_partner(): return lax.ppermute(block, 'cp', [(i, i ^ mask) for i in range(size)])  13.9 us
    ppermute x6, starting transfers between devices, to_partner(): return lax.ppermute(block, 'cp', [(i, i ^ mask) for i in range(size)])  11.4 us
    pallas_call x4, Pallas kernels, unpack_rows(): pl.pallas_call(kernel, in_specs=in_specs, out_specs=specs(pl.ANY, 1) + sp...  10.4 us
    unnamed x24, local copies, waits for them, and re-layouts  6.84 us
  transfers between devices with their start and end apart: 26, of which 8 were waited for; matrix products, arithmetic and copies ran while one was open for 0% of the time, Pallas kernels for 19%

profile of v2, /device:TPU:0, one launch (start us, length us, event | category | flops | bytes accessed | tf_op | source)
XLA Modules:
  0.0 136.9 jit_solution(9846965024534148835)
XLA Ops:
  1.9 3.1 %collective-permute-start.3 = (bf16[128,768]{1,0:T(8,128)(2,1)S(1)}, bf16[128,768]{1,0:T(8,128)(2,1)S(1)}, u32[]{:S(2)}, u32[]{:S(2)}) collective-permute-start(bf16[128,768]{1,0:T(8,128)(2,1)S(1)} %get-tuple-element.41.refs_0_), channel_id=1, source_target_pairs={{0,2},{2,0},{4,6},{6,4},{1,3},{3,1},{5,7},{7,5},{8,10},{10,8},{12,... | collective-permute-start | bytes 589832 | tf_op jit(solution)/shard_map/ppermute | solution.py:125
  5.0 2.6 %collective-permute-start.4 = (bf16[128,768]{1,0:T(8,128)(2,1)S(1)}, bf16[128,768]{1,0:T(8,128)(2,1)S(1)}, u32[]{:S(2)}, u32[]{:S(2)}) collective-permute-start(bf16[128,768]{1,0:T(8,128)(2,1)S(1)} %get-tuple-element.41.refs_0_), channel_id=1, source_target_pairs={{0,4},{2,6},{4,0},{6,2},{1,5},{3,7},{5,1},{7,3},{8,12},{10,14},{12... | collective-permute-start | bytes 589832 | tf_op jit(solution)/shard_map/ppermute | solution.py:125
  8.0 3.9 %collective-permute-start.2 = (bf16[144,256]{1,0:T(8,128)(2,1)S(1)}, bf16[144,256]{1,0:T(8,128)(2,1)S(1)}, u32[]{:S(2)}, u32[]{:S(2)}) collective-permute-start(bf16[144,256]{1,0:T(8,128)(2,1)S(1)} %get-tuple-element.40.refs_0_), channel_id=1, source_target_pairs={{0,6},{2,4},{4,2},{6,0},{1,7},{3,5},{5,3},{7,1},{8,14},{10,12},{12... | collective-permute-start | bytes 221192 | tf_op jit(solution)/shard_map/ppermute | solution.py:125
  11.9 4.2 %collective-permute-done.refs_1_.refs_0_ = bf16[144,256]{1,0:T(8,128)(2,1)S(1)} collective-permute-done((bf16[144,256]{1,0:T(8,128)(2,1)S(1)}, bf16[144,256]{1,0:T(8,128)(2,1)S(1)}, u32[]{:S(2)}, u32[]{:S(2)}) %collective-permute-start) | collective-permute-done | bytes 73760 | tf_op jit(solution)/shard_map/ppermute | solution.py:125
  16.1 5.9 %collective-permute-done.1.refs_2_.refs_1_ = bf16[144,256]{1,0:T(8,128)(2,1)S(1)} collective-permute-done((bf16[144,256]{1,0:T(8,128)(2,1)S(1)}, bf16[144,256]{1,0:T(8,128)(2,1)S(1)}, u32[]{:S(2)}, u32[]{:S(2)}) %collective-permute-start.1) | collective-permute-done | bytes 73760 | tf_op jit(solution)/shard_map/ppermute | solution.py:125
  23.6 4.1 %attend.4 = (bf16[64,2048]{1,0:T(8,128)(2,1)S(1)}, bf16[64,2048]{1,0:T(8,128)(2,1)S(1)}, bf16[64,2048]{1,0:T(8,128)(2,1)S(1)}, bf16[64,2048]{1,0:T(8,128)(2,1)S(1)}) custom-call(bf16[128,8192]{1,0:T(8,128)(2,1)S(1)} %copy-done, bf16[512,256]{1,0:T(8,128)(2,1)S(1)} %get-tuple-element.38.pack_ref, f32[2,256,128]{2,1,0:T(8,128)S(1)} %get-tuple-element.39.allow_ref, ...), custom_call_target="tpu_custom_call" | custom-call | tf_op jit(solution)/shard_map/attend/pallas_call | solution.py:320
  32.2 3.3 %collective-permute-start.7 = (bf16[64,2048]{1,0:T(8,128)(2,1)S(1)}, bf16[64,2048]{1,0:T(8,128)(2,1)S(1)}, u32[]{:S(2)}, u32[]{:S(2)}) collective-permute-start(bf16[64,2048]{1,0:T(8,128)(2,1)S(1)} %get-tuple-element.47), channel_id=1, source_target_pairs={{0,12},{2,14},{4,8},{6,10},{8,20},{10,22},{12,16},{14,18},{16,28},... | collective-permute-start | bytes 786440 | tf_op jit(solution)/shard_map/ppermute | solution.py:135
  36.8 3.8 %collective-permute-done.10.refs_3_ = bf16[128,768]{1,0:T(8,128)(2,1)S(1)} collective-permute-done((bf16[128,768]{1,0:T(8,128)(2,1)S(1)}, bf16[128,768]{1,0:T(8,128)(2,1)S(1)}, u32[]{:S(2)}, u32[]{:S(2)}) %collective-permute-start.10) | collective-permute-done | bytes 196640 | tf_op jit(solution)/shard_map/ppermute | solution.py:125
  40.6 4.1 %attend.5 = (bf16[64,2048]{1,0:T(8,128)(2,1)S(1)}, bf16[64,2048]{1,0:T(8,128)(2,1)S(1)}, bf16[64,2048]{1,0:T(8,128)(2,1)S(1)}, bf16[64,2048]{1,0:T(8,128)(2,1)S(1)}) custom-call(bf16[128,8192]{1,0:T(8,128)(2,1)S(1)} %copy-done.1, bf16[512,256]{1,0:T(8,128)(2,1)S(1)} %get-tuple-element.38.pack_ref, f32[2,256,128]{2,1,0:T(8,128)S(1)} %get-tuple-element.39.allow_ref, ...), custom_call_target="tpu_custom_call" | custom-call | tf_op jit(solution)/shard_map/attend/pallas_call | solution.py:320
  46.9 2.9 %collective-permute-done.5.refs_0_ = bf16[64,2048]{1,0:T(8,128)(2,1)S(1)} collective-permute-done((bf16[64,2048]{1,0:T(8,128)(2,1)S(1)}, bf16[64,2048]{1,0:T(8,128)(2,1)S(1)}, u32[]{:S(2)}, u32[]{:S(2)}) %collective-permute-start.5) | collective-permute-done | bytes 262176 | tf_op jit(solution)/shard_map/ppermute | solution.py:135
  51.9 4.8 %attend.6 = (bf16[64,2048]{1,0:T(8,128)(2,1)S(1)}, bf16[64,2048]{1,0:T(8,128)(2,1)S(1)}, bf16[64,2048]{1,0:T(8,128)(2,1)S(1)}, bf16[64,2048]{1,0:T(8,128)(2,1)}) custom-call(bf16[128,8192]{1,0:T(8,128)(2,1)S(1)} %copy-done.1, bf16[512,256]{1,0:T(8,128)(2,1)S(1)} %get-tuple-element.38.pack_ref, f32[2,256,128]{2,1,0:T(8,128)S(1)} %get-tuple-element.39.allow_ref, ...), custom_call_target="tpu_custom_call" | custom-call | tf_op jit(solution)/shard_map/attend/pallas_call | solution.py:320
  56.8 4.7 %collective-permute-start.13 = (bf16[64,2048]{1,0:T(8,128)(2,1)S(1)}, bf16[64,2048]{1,0:T(8,128)(2,1)S(1)}, u32[]{:S(2)}, u32[]{:S(2)}) collective-permute-start(bf16[64,2048]{1,0:T(8,128)(2,1)S(1)} %get-tuple-element.54), channel_id=1, source_target_pairs={{0,12},{2,14},{4,8},{6,10},{8,20},{10,22},{12,16},{14,18},{16,28},... | collective-permute-start | bytes 786440 | tf_op jit(solution)/shard_map/ppermute | solution.py:135
  61.4 5.9 %collective-permute-start.14 = (bf16[64,2048]{1,0:T(8,128)(2,1)S(1)}, bf16[64,2048]{1,0:T(8,128)(2,1)S(1)}, u32[]{:S(2)}, u32[]{:S(2)}) collective-permute-start(bf16[64,2048]{1,0:T(8,128)(2,1)S(1)} %get-tuple-element.55), channel_id=1, source_target_pairs={{0,14},{2,12},{4,10},{6,8},{8,22},{10,20},{12,18},{14,16},{16,30},... | collective-permute-start | bytes 786440 | tf_op jit(solution)/shard_map/ppermute | solution.py:135
  68.5 7.0 %collective-permute-start.17 = (bf16[64,2048]{1,0:T(8,128)(2,1)S(1)}, bf16[64,2048]{1,0:T(8,128)(2,1)S(1)}, u32[]{:S(2)}, u32[]{:S(2)}) collective-permute-start(bf16[64,2048]{1,0:T(8,128)(2,1)S(1)} %get-tuple-element.59), channel_id=1, source_target_pairs={{0,10},{2,8},{4,14},{6,12},{8,18},{10,16},{12,22},{14,20},{16,26},... | collective-permute-start | bytes 786440 | tf_op jit(solution)/shard_map/ppermute | solution.py:135
  75.5 2.5 %collective-permute-start.18 = (bf16[64,2048]{1,0:T(8,128)(2,1)S(1)}, bf16[64,2048]{1,0:T(8,128)(2,1)S(1)}, u32[]{:S(2)}, u32[]{:S(2)}) collective-permute-start(bf16[64,2048]{1,0:T(8,128)(2,1)S(1)} %get-tuple-element.60), channel_id=1, source_target_pairs={{0,12},{2,14},{4,8},{6,10},{8,20},{10,22},{12,16},{14,18},{16,28},... | collective-permute-start | bytes 786440 | tf_op jit(solution)/shard_map/ppermute | solution.py:135
  78.0 5.0 %attend.7 = (bf16[64,2048]{1,0:T(8,128)(2,1)}, bf16[64,2048]{1,0:T(8,128)(2,1)}, bf16[64,2048]{1,0:T(8,128)(2,1)}, bf16[64,2048]{1,0:T(8,128)(2,1)}) custom-call(bf16[128,8192]{1,0:T(8,128)(2,1)S(1)} %copy-done.1, bf16[512,256]{1,0:T(8,128)(2,1)S(1)} %get-tuple-element.38.pack_ref, f32[2,256,128]{2,1,0:T(8,128)S(1)} %get-tuple-element.39.allow_ref, ...), custom_call_target="tpu_custom_call" | custom-call | tf_op jit(solution)/shard_map/attend/pallas_call | solution.py:320
  83.1 3.5 %collective-permute-start.19 = (bf16[64,2048]{1,0:T(8,128)(2,1)}, bf16[64,2048]{1,0:T(8,128)(2,1)}, u32[]{:S(2)}, u32[]{:S(2)}) collective-permute-start(bf16[64,2048]{1,0:T(8,128)(2,1)} %get-tuple-element.61), channel_id=1, source_target_pairs={{0,14},{2,12},{4,10},{6,8},{8,22},{10,20},{12,18},{14,16},{16,30},... | collective-permute-start | bytes 786440 | tf_op jit(solution)/shard_map/ppermute | solution.py:135
  86.8 11.5 %collective-permute-done.16.refs_0_ = bf16[64,2048]{1,0:T(8,128)(2,1)S(1)} collective-permute-done((bf16[64,2048]{1,0:T(8,128)(2,1)S(1)}, bf16[64,2048]{1,0:T(8,128)(2,1)S(1)}, u32[]{:S(2)}, u32[]{:S(2)}) %collective-permute-start.16) | collective-permute-done | bytes 262176 | tf_op jit(solution)/shard_map/ppermute | solution.py:135
  101.0 8.9 %collective-permute-done.18.refs_2_ = bf16[64,2048]{1,0:T(8,128)(2,1)S(1)} collective-permute-done((bf16[64,2048]{1,0:T(8,128)(2,1)S(1)}, bf16[64,2048]{1,0:T(8,128)(2,1)S(1)}, u32[]{:S(2)}, u32[]{:S(2)}) %collective-permute-start.18) | collective-permute-done | bytes 262176 | tf_op jit(solution)/shard_map/ppermute | solution.py:135
  110.7 5.4 %collective-permute-start.24 = (bf16[64,2048]{1,0:T(8,128)(2,1)}, bf16[64,2048]{1,0:T(8,128)(2,1)}, u32[]{:S(2)}, u32[]{:S(2)}) collective-permute-start(bf16[64,2048]{1,0:T(8,128)(2,1)} %get-tuple-element.67), channel_id=1, source_target_pairs={{0,14},{2,12},{4,10},{6,8},{8,22},{10,20},{12,18},{14,16},{16,30},... | collective-permute-start | bytes 786440 | tf_op jit(solution)/shard_map/ppermute | solution.py:135
  121.1 2.6 %unpack_rows.4 = (bf16[128,16384]{1,0:T(8,128)(2,1)}, bf16[128,2048]{1,0:T(8,128)(2,1)}) custom-call(s32[3]{0:T(128)} %pad_add_fusion.where_ref, bf16[64,2048]{1,0:T(8,128)(2,1)S(1)} %copy-done.5, bf16[64,2048]{1,0:T(8,128)(2,1)S(1)} %copy-done.7, bf16[64,2048]{1,0:T(8,128)(2,1)S(1)} %copy-done.9, bf16[64,2048]{1,0:T(8,128)(2,1)S(1)} %copy-done.11, ...), custom_call_target="tpu_custom_call" | custom-call | tf_op jit(solution)/shard_map/unpack_rows/pallas_call | solution.py:365
  123.7 2.7 %unpack_rows.5 = (bf16[128,16384]{1,0:T(8,128)(2,1)}, bf16[128,2048]{1,0:T(8,128)(2,1)}) custom-call(s32[3]{0:T(128)} %pad_add_fusion.where_ref, bf16[64,2048]{1,0:T(8,128)(2,1)S(1)} %collective-permute-done.11.refs_0_, bf16[64,2048]{1,0:T(8,128)(2,1)S(1)} %collective-permute-done.12.refs_1_, ...), custom_call_target="tpu_custom_call", output_to_operand_aliasing={{0}: (6, {})} | custom-call | tf_op jit(solution)/shard_map/unpack_rows/pallas_call | solution.py:365
  126.5 2.9 %unpack_rows.6 = (bf16[128,16384]{1,0:T(8,128)(2,1)}, bf16[128,2048]{1,0:T(8,128)(2,1)}) custom-call(s32[3]{0:T(128)} %pad_add_fusion.where_ref, bf16[64,2048]{1,0:T(8,128)(2,1)S(1)} %collective-permute-done.16.refs_0_, bf16[64,2048]{1,0:T(8,128)(2,1)S(1)} %collective-permute-done.17.refs_1_, ...), custom_call_target="tpu_custom_call", output_to_operand_aliasing={{0}: (6, {})} | custom-call | tf_op jit(solution)/shard_map/unpack_rows/pallas_call | solution.py:365
  134.4 2.4 %place_twins.1 = bf16[128,16384]{1,0:T(8,128)(2,1)} custom-call(s32[3]{0:T(128)} %pad_add_fusion.where_ref, bf16[128,2048]{1,0:T(8,128)(2,1)S(1)} %collective-permute-done.9.refs_0_, bf16[128,2048]{1,0:T(8,128)(2,1)S(1)} %collective-permute-done.15.refs_1_, bf16[128,2048]{1,0:T(8,128)(2,1)} %collective-permute-done.20.refs_2_, ...), custom_call_target="tpu_custom_call", output_to_operand_aliasing={{}: (5, {})} | custom-call | tf_op jit(solution)/shard_map/place_twins/pallas_call | solution.py:392
  (64 shorter events, 28.9 us)
Async XLA Ops:
  1.9 20.1 %collective-permute-start.3 = (bf16[128,768]{1,0:T(8,128)(2,1)S(1)}, bf16[128,768]{1,0:T(8,128)(2,1)S(1)}, u32[]{:S(2)}, u32[]{:S(2)}) collective-permute-start(bf16[128,768]{1,0:T(8,128)(2,1)S(1)} %get-tuple-element.41.refs_0_), channel_id=1, source_target_pairs={{0,2},{2,0},{4,6},{6,4},{1,3},{3,1},{5,7},{7,5},{8,10},{10,8},{12,... | collective-permute-start | bytes 589832 | tf_op jit(solution)/shard_map/ppermute | solution.py:125
  5.0 17.1 %collective-permute-start.4 = (bf16[128,768]{1,0:T(8,128)(2,1)S(1)}, bf16[128,768]{1,0:T(8,128)(2,1)S(1)}, u32[]{:S(2)}, u32[]{:S(2)}) collective-permute-start(bf16[128,768]{1,0:T(8,128)(2,1)S(1)} %get-tuple-element.41.refs_0_), channel_id=1, source_target_pairs={{0,4},{2,6},{4,0},{6,2},{1,5},{3,7},{5,1},{7,3},{8,12},{10,14},{12... | collective-permute-start | bytes 589832 | tf_op jit(solution)/shard_map/ppermute | solution.py:125
  7.5 8.6 %collective-permute-start = (bf16[144,256]{1,0:T(8,128)(2,1)S(1)}, bf16[144,256]{1,0:T(8,128)(2,1)S(1)}, u32[]{:S(2)}, u32[]{:S(2)}) collective-permute-start(bf16[144,256]{1,0:T(8,128)(2,1)S(1)} %get-tuple-element.40.refs_0_), channel_id=1, source_target_pairs={{0,2},{2,0},{4,6},{6,4},{1,3},{3,1},{5,7},{7,5},{8,10},{10,8},{12,... | collective-permute-start | bytes 221192 | tf_op jit(solution)/shard_map/ppermute | solution.py:125
  8.0 14.0 %collective-permute-start.1 = (bf16[144,256]{1,0:T(8,128)(2,1)S(1)}, bf16[144,256]{1,0:T(8,128)(2,1)S(1)}, u32[]{:S(2)}, u32[]{:S(2)}) collective-permute-start(bf16[144,256]{1,0:T(8,128)(2,1)S(1)} %get-tuple-element.40.refs_0_), channel_id=1, source_target_pairs={{0,4},{2,6},{4,0},{6,2},{1,5},{3,7},{5,1},{7,3},{8,12},{10,14},{12... | collective-permute-start | bytes 221192 | tf_op jit(solution)/shard_map/ppermute | solution.py:125
  8.0 14.0 %collective-permute-start.2 = (bf16[144,256]{1,0:T(8,128)(2,1)S(1)}, bf16[144,256]{1,0:T(8,128)(2,1)S(1)}, u32[]{:S(2)}, u32[]{:S(2)}) collective-permute-start(bf16[144,256]{1,0:T(8,128)(2,1)S(1)} %get-tuple-element.40.refs_0_), channel_id=1, source_target_pairs={{0,6},{2,4},{4,2},{6,0},{1,7},{3,5},{5,3},{7,1},{8,14},{10,12},{12... | collective-permute-start | bytes 221192 | tf_op jit(solution)/shard_map/ppermute | solution.py:125
  27.7 22.0 %collective-permute-start.5 = (bf16[64,2048]{1,0:T(8,128)(2,1)S(1)}, bf16[64,2048]{1,0:T(8,128)(2,1)S(1)}, u32[]{:S(2)}, u32[]{:S(2)}) collective-permute-start(bf16[64,2048]{1,0:T(8,128)(2,1)S(1)} %get-tuple-element.45), channel_id=1, source_target_pairs={{0,8},{2,10},{4,12},{6,14},{8,16},{10,18},{12,20},{14,22},{16,24},... | collective-permute-start | bytes 786440 | tf_op jit(solution)/shard_map/ppermute | solution.py:135
  29.3 11.3 %collective-permute-start.10 = (bf16[128,768]{1,0:T(8,128)(2,1)S(1)}, bf16[128,768]{1,0:T(8,128)(2,1)S(1)}, u32[]{:S(2)}, u32[]{:S(2)}) collective-permute-start(bf16[128,768]{1,0:T(8,128)(2,1)S(1)} %collective-permute-done.4.refs_2_), channel_id=1, source_target_pairs={{0,2},{2,0},{4,6},{6,4},{1,3},{3,1},{5,7},{7,5},{8,10},{10,8},{12,... | collective-permute-start | bytes 589832 | tf_op jit(solution)/shard_map/ppermute | solution.py:125
  30.6 26.1 %collective-permute-start.6 = (bf16[64,2048]{1,0:T(8,128)(2,1)S(1)}, bf16[64,2048]{1,0:T(8,128)(2,1)S(1)}, u32[]{:S(2)}, u32[]{:S(2)}) collective-permute-start(bf16[64,2048]{1,0:T(8,128)(2,1)S(1)} %get-tuple-element.46), channel_id=1, source_target_pairs={{0,10},{2,8},{4,14},{6,12},{8,18},{10,16},{12,22},{14,20},{16,26},... | collective-permute-start | bytes 786440 | tf_op jit(solution)/shard_map/ppermute | solution.py:135
  32.2 29.2 %collective-permute-start.7 = (bf16[64,2048]{1,0:T(8,128)(2,1)S(1)}, bf16[64,2048]{1,0:T(8,128)(2,1)S(1)}, u32[]{:S(2)}, u32[]{:S(2)}) collective-permute-start(bf16[64,2048]{1,0:T(8,128)(2,1)S(1)} %get-tuple-element.47), channel_id=1, source_target_pairs={{0,12},{2,14},{4,8},{6,10},{8,20},{10,22},{12,16},{14,18},{16,28},... | collective-permute-start | bytes 786440 | tf_op jit(solution)/shard_map/ppermute | solution.py:135
  35.5 31.9 %collective-permute-start.8 = (bf16[64,2048]{1,0:T(8,128)(2,1)S(1)}, bf16[64,2048]{1,0:T(8,128)(2,1)S(1)}, u32[]{:S(2)}, u32[]{:S(2)}) collective-permute-start(bf16[64,2048]{1,0:T(8,128)(2,1)S(1)} %get-tuple-element.48), channel_id=1, source_target_pairs={{0,14},{2,12},{4,10},{6,8},{8,22},{10,20},{12,18},{14,16},{16,30},... | collective-permute-start | bytes 786440 | tf_op jit(solution)/shard_map/ppermute | solution.py:135
  44.7 23.8 %collective-permute-start.11 = (bf16[64,2048]{1,0:T(8,128)(2,1)S(1)}, bf16[64,2048]{1,0:T(8,128)(2,1)S(1)}, u32[]{:S(2)}, u32[]{:S(2)}) collective-permute-start(bf16[64,2048]{1,0:T(8,128)(2,1)S(1)} %get-tuple-element.52), channel_id=1, source_target_pairs={{0,8},{2,10},{4,12},{6,14},{8,16},{10,18},{12,20},{14,22},{16,24},... | collective-permute-start | bytes 786440 | tf_op jit(solution)/shard_map/ppermute | solution.py:135
  49.7 25.8 %collective-permute-start.12 = (bf16[64,2048]{1,0:T(8,128)(2,1)S(1)}, bf16[64,2048]{1,0:T(8,128)(2,1)S(1)}, u32[]{:S(2)}, u32[]{:S(2)}) collective-permute-start(bf16[64,2048]{1,0:T(8,128)(2,1)S(1)} %get-tuple-element.53), channel_id=1, source_target_pairs={{0,10},{2,8},{4,14},{6,12},{8,18},{10,16},{12,22},{14,20},{16,26},... | collective-permute-start | bytes 786440 | tf_op jit(solution)/shard_map/ppermute | solution.py:135
  56.8 26.3 %collective-permute-start.13 = (bf16[64,2048]{1,0:T(8,128)(2,1)S(1)}, bf16[64,2048]{1,0:T(8,128)(2,1)S(1)}, u32[]{:S(2)}, u32[]{:S(2)}) collective-permute-start(bf16[64,2048]{1,0:T(8,128)(2,1)S(1)} %get-tuple-element.54), channel_id=1, source_target_pairs={{0,12},{2,14},{4,8},{6,10},{8,20},{10,22},{12,16},{14,18},{16,28},... | collective-permute-start | bytes 786440 | tf_op jit(solution)/shard_map/ppermute | solution.py:135
  61.4 25.1 %collective-permute-start.14 = (bf16[64,2048]{1,0:T(8,128)(2,1)S(1)}, bf16[64,2048]{1,0:T(8,128)(2,1)S(1)}, u32[]{:S(2)}, u32[]{:S(2)}) collective-permute-start(bf16[64,2048]{1,0:T(8,128)(2,1)S(1)} %get-tuple-element.55), channel_id=1, source_target_pairs={{0,14},{2,12},{4,10},{6,8},{8,22},{10,20},{12,18},{14,16},{16,30},... | collective-permute-start | bytes 786440 | tf_op jit(solution)/shard_map/ppermute | solution.py:135
  68.1 30.2 %collective-permute-start.16 = (bf16[64,2048]{1,0:T(8,128)(2,1)S(1)}, bf16[64,2048]{1,0:T(8,128)(2,1)S(1)}, u32[]{:S(2)}, u32[]{:S(2)}) collective-permute-start(bf16[64,2048]{1,0:T(8,128)(2,1)S(1)} %get-tuple-element.58), channel_id=1, source_target_pairs={{0,8},{2,10},{4,12},{6,14},{8,16},{10,18},{12,20},{14,22},{16,24},... | collective-permute-start | bytes 786440 | tf_op jit(solution)/shard_map/ppermute | solution.py:135
  68.5 31.4 %collective-permute-start.17 = (bf16[64,2048]{1,0:T(8,128)(2,1)S(1)}, bf16[64,2048]{1,0:T(8,128)(2,1)S(1)}, u32[]{:S(2)}, u32[]{:S(2)}) collective-permute-start(bf16[64,2048]{1,0:T(8,128)(2,1)S(1)} %get-tuple-element.59), channel_id=1, source_target_pairs={{0,10},{2,8},{4,14},{6,12},{8,18},{10,16},{12,22},{14,20},{16,26},... | collective-permute-start | bytes 786440 | tf_op jit(solution)/shard_map/ppermute | solution.py:135
  75.5 34.4 %collective-permute-start.18 = (bf16[64,2048]{1,0:T(8,128)(2,1)S(1)}, bf16[64,2048]{1,0:T(8,128)(2,1)S(1)}, u32[]{:S(2)}, u32[]{:S(2)}) collective-permute-start(bf16[64,2048]{1,0:T(8,128)(2,1)S(1)} %get-tuple-element.60), channel_id=1, source_target_pairs={{0,12},{2,14},{4,8},{6,10},{8,20},{10,22},{12,16},{14,18},{16,28},... | collective-permute-start | bytes 786440 | tf_op jit(solution)/shard_map/ppermute | solution.py:135
  83.1 43.4 %collective-permute-start.19 = (bf16[64,2048]{1,0:T(8,128)(2,1)}, bf16[64,2048]{1,0:T(8,128)(2,1)}, u32[]{:S(2)}, u32[]{:S(2)}) collective-permute-start(bf16[64,2048]{1,0:T(8,128)(2,1)} %get-tuple-element.61), channel_id=1, source_target_pairs={{0,14},{2,12},{4,10},{6,8},{8,22},{10,20},{12,18},{14,16},{16,30},... | collective-permute-start | bytes 786440 | tf_op jit(solution)/shard_map/ppermute | solution.py:135
  86.6 42.9 %collective-permute-start.21 = (bf16[64,2048]{1,0:T(8,128)(2,1)}, bf16[64,2048]{1,0:T(8,128)(2,1)}, u32[]{:S(2)}, u32[]{:S(2)}) collective-permute-start(bf16[64,2048]{1,0:T(8,128)(2,1)} %get-tuple-element.64), channel_id=1, source_target_pairs={{0,8},{2,10},{4,12},{6,14},{8,16},{10,18},{12,20},{14,22},{16,24},... | collective-permute-start | bytes 786440 | tf_op jit(solution)/shard_map/ppermute | solution.py:135
  98.3 31.7 %collective-permute-start.22 = (bf16[64,2048]{1,0:T(8,128)(2,1)}, bf16[64,2048]{1,0:T(8,128)(2,1)}, u32[]{:S(2)}, u32[]{:S(2)}) collective-permute-start(bf16[64,2048]{1,0:T(8,128)(2,1)} %get-tuple-element.65), channel_id=1, source_target_pairs={{0,10},{2,8},{4,14},{6,12},{8,18},{10,16},{12,22},{14,20},{16,26},... | collective-permute-start | bytes 786440 | tf_op jit(solution)/shard_map/ppermute | solution.py:135
  99.9 30.2 %collective-permute-start.23 = (bf16[64,2048]{1,0:T(8,128)(2,1)}, bf16[64,2048]{1,0:T(8,128)(2,1)}, u32[]{:S(2)}, u32[]{:S(2)}) collective-permute-start(bf16[64,2048]{1,0:T(8,128)(2,1)} %get-tuple-element.66), channel_id=1, source_target_pairs={{0,12},{2,14},{4,8},{6,10},{8,20},{10,22},{12,16},{14,18},{16,28},... | collective-permute-start | bytes 786440 | tf_op jit(solution)/shard_map/ppermute | solution.py:135
  110.7 19.4 %collective-permute-start.24 = (bf16[64,2048]{1,0:T(8,128)(2,1)}, bf16[64,2048]{1,0:T(8,128)(2,1)}, u32[]{:S(2)}, u32[]{:S(2)}) collective-permute-start(bf16[64,2048]{1,0:T(8,128)(2,1)} %get-tuple-element.67), channel_id=1, source_target_pairs={{0,14},{2,12},{4,10},{6,8},{8,22},{10,20},{12,18},{14,16},{16,30},... | collective-permute-start | bytes 786440 | tf_op jit(solution)/shard_map/ppermute | solution.py:135
  126.4 6.4 %collective-permute-start.9 = (bf16[128,2048]{1,0:T(8,128)(2,1)}, bf16[128,2048]{1,0:T(8,128)(2,1)S(1)}, u32[]{:S(2)}, u32[]{:S(2)}) collective-permute-start(bf16[128,2048]{1,0:T(8,128)(2,1)} %get-tuple-element.49), channel_id=1, source_target_pairs={{0,1},{1,0},{2,3},{3,2},{4,5},{5,4},{6,7},{7,6},{8,9},{9,8},{10,11... | collective-permute-start | bytes 1572872 | tf_op jit(solution)/shard_map/ppermute | solution.py:438
  129.4 3.4 %collective-permute-start.15 = (bf16[128,2048]{1,0:T(8,128)(2,1)}, bf16[128,2048]{1,0:T(8,128)(2,1)S(1)}, u32[]{:S(2)}, u32[]{:S(2)}) collective-permute-start(bf16[128,2048]{1,0:T(8,128)(2,1)} %get-tuple-element.57), channel_id=1, source_target_pairs={{0,1},{1,0},{2,3},{3,2},{4,5},{5,4},{6,7},{7,6},{8,9},{9,8},{10,11... | collective-permute-start | bytes 1572872 | tf_op jit(solution)/shard_map/ppermute | solution.py:438
  (14 other events, 165.9 us)
